TPU v7x, 32 devices: a whole 2x2x4 slice. The times are simulated.
32 devices in a mesh: fsdp: 32 (over z, y, x, core).
Axes of the slice: x: 2, y: 2, z: 4, core: 2. Of those that a mesh axis runs over, the one named last changes fastest.
Arguments:
- decoder_in: bfloat16 [65536, 512], P('fsdp'), may hold values from -12 to 12
- memory: bfloat16 [16384, 512], P('fsdp'), may hold values from -12 to 12
- cotangent: bfloat16 [65536, 512], P('fsdp'), may hold values from -12 to 12
- self_query: bfloat16 [512, 512], P('fsdp'), may hold values from -0.25 to 0.25
- self_query_bias: bfloat16 [512], P('fsdp'), may hold values from -1.25 to 1.25
- self_key: bfloat16 [512, 512], P('fsdp'), may hold values from -0.25 to 0.25
- self_value: bfloat16 [512, 512], P('fsdp'), may hold values from -0.25 to 0.25
- self_value_bias: bfloat16 [512], P('fsdp'), may hold values from -1.25 to 1.25
- self_output: bfloat16 [512, 512], P('fsdp'), may hold values from -2 to 2
- self_output_bias: bfloat16 [512], P('fsdp'), may hold values from -1.25 to 1.25
- first_gain: bfloat16 [512], P('fsdp'), may hold values from 0.5 to 1.5
- first_shift: bfloat16 [512], P('fsdp'), may hold values from -1.25 to 1.25
- cross_query: bfloat16 [512, 512], P('fsdp'), may hold values from -0.25 to 0.25
- cross_query_bias: bfloat16 [512], P('fsdp'), may hold values from -1.25 to 1.25
- cross_key: bfloat16 [512, 512], P('fsdp'), may hold values from -0.25 to 0.25
- cross_value: bfloat16 [512, 512], P('fsdp'), may hold values from -0.25 to 0.25
- cross_value_bias: bfloat16 [512], P('fsdp'), may hold values from -1.25 to 1.25
- cross_output: bfloat16 [512, 512], P('fsdp'), may hold values from -2 to 2
- cross_output_bias: bfloat16 [512], P('fsdp'), may hold values from -1.25 to 1.25
- second_gain: bfloat16 [512], P('fsdp'), may hold values from 0.5 to 1.5
- second_shift: bfloat16 [512], P('fsdp'), may hold values from -1.25 to 1.25
- expand_weight: bfloat16 [512, 2048], P('fsdp'), may hold values from -0.25 to 0.25
- expand_bias: bfloat16 [2048], P('fsdp'), may hold values from -1.25 to 1.25
- contract_weight: bfloat16 [2048, 512], P('fsdp'), may hold values from -0.25 to 0.25
- contract_bias: bfloat16 [512], P('fsdp'), may hold values from -1.25 to 1.25
- third_gain: bfloat16 [512], P('fsdp'), may hold values from 0.5 to 1.5
- third_shift: bfloat16 [512], P('fsdp'), may hold values from -1.25 to 1.25
Outputs:
- decoder_out: bfloat16 [65536, 512], P('fsdp')
- input_grad: float32 [65536, 512], P('fsdp')
- memory_grad: float32 [16384, 512], P('fsdp')
- self_query_grad: float32 [512, 512], P('fsdp')
- self_query_bias_grad: float32 [512], P('fsdp')
- self_key_grad: float32 [512, 512], P('fsdp')
- self_value_grad: float32 [512, 512], P('fsdp')
- self_value_bias_grad: float32 [512], P('fsdp')
- self_output_grad: float32 [512, 512], P('fsdp')
- self_output_bias_grad: float32 [512], P('fsdp')
- first_gain_grad: float32 [512], P('fsdp')
- first_shift_grad: float32 [512], P('fsdp')
- cross_query_grad: float32 [512, 512], P('fsdp')
- cross_query_bias_grad: float32 [512], P('fsdp')
- cross_key_grad: float32 [512, 512], P('fsdp')
- cross_value_grad: float32 [512, 512], P('fsdp')
- cross_value_bias_grad: float32 [512], P('fsdp')
- cross_output_grad: float32 [512, 512], P('fsdp')
- cross_output_bias_grad: float32 [512], P('fsdp')
- second_gain_grad: float32 [512], P('fsdp')
- second_shift_grad: float32 [512], P('fsdp')
- expand_weight_grad: float32 [512, 2048], P('fsdp')
- expand_bias_grad: float32 [2048], P('fsdp')
- contract_weight_grad: float32 [2048, 512], P('fsdp')
- contract_bias_grad: float32 [512], P('fsdp')
- third_gain_grad: float32 [512], P('fsdp')
- third_shift_grad: float32 [512], P('fsdp')
All inputs are finite; a program needn't handle non-finite values.
Results may differ from a plain program's by a relative error of at most 0.03.
Values may be sent and summed in bfloat16 or wider, within the bound.
No kernel may reach another device: no remote copies, remote signals or barrier semaphores. Data moves between devices by JAX's collectives and lax.ppermute only.
A program may use at most 384 MiB of HBM per device.

v0:
```python
import jax
import jax.numpy as jnp
from jax import lax
from jax.sharding import PartitionSpec as P

HEADS = 8


epsilon = 1e-05


def project(activ, weight, bias):
    result = jnp.dot(activ, weight, preferred_element_type=jnp.float32)
    if bias is None:
        return result
    return result + bias.astype(jnp.float32)


def weight_grad(activ, grad_low):
    return lax.dot_general(
        activ, grad_low, (((0,), (0,)), ((), ())), preferred_element_type=jnp.float32
    )


def back_proj(grad_low, weight):
    return lax.dot_general(
        grad_low, weight, (((1,), (1,)), ((), ())), preferred_element_type=jnp.float32
    )


def column_sum(grad_low):
    return jnp.sum(grad_low, axis=0, dtype=jnp.float32)


def layer_norm(summed, gain, shift):
    row_mean = jnp.mean(summed, axis=-1, keepdims=True)
    centred = summed - row_mean
    variance = jnp.mean(centred * centred, axis=-1, keepdims=True)
    inverse = lax.rsqrt(variance + epsilon)
    normed = centred * inverse
    return (normed * gain.astype(jnp.float32) + shift.astype(jnp.float32), normed, inverse)


def norm_back(incoming, normed, inverse, gain):
    gain_grad = jnp.sum(incoming * normed, axis=0)
    shift_grad = jnp.sum(incoming, axis=0)
    scaled = incoming * gain.astype(jnp.float32)
    summed_grad = inverse * (
        scaled
        - jnp.mean(scaled, axis=-1, keepdims=True)
        - normed * jnp.mean(scaled * normed, axis=-1, keepdims=True)
    )
    return (gain_grad, shift_grad, summed_grad)


def block_scores(query_block, key_block, row_start, causal, score_scale):
    scores = (
        jnp.einsum("qhd,khd->hqk", query_block, key_block, preferred_element_type=jnp.float32)
        * score_scale
    )
    if causal:
        rows_here = query_block.shape[0]
        allowed = (
            lax.broadcasted_iota(jnp.int32, (rows_here, key_block.shape[0]), 1)
            <= lax.broadcasted_iota(jnp.int32, (rows_here, key_block.shape[0]), 0) + row_start
        )
        scores = jnp.where(allowed[None], scores, -1e30)
    return scores


def attend_forward(query_low, key_low, value_low, causal):
    length, model_width = query_low.shape
    keys_count = key_low.shape[0]
    head_dim = model_width // HEADS
    score_scale = head_dim ** (-0.5)
    block_rows = min(512, length)
    query_heads = query_low.reshape(length, HEADS, head_dim)
    key_heads = key_low.reshape(keys_count, HEADS, head_dim)
    value_heads = value_low.reshape(keys_count, HEADS, head_dim)
    pieces = []
    log_sums = []
    for row_start in range(0, length, block_rows):
        key_end = row_start + block_rows if causal else keys_count
        scores = block_scores(
            query_heads[row_start : row_start + block_rows],
            key_heads[:key_end],
            row_start,
            causal,
            score_scale,
        )
        row_peak = jnp.max(scores, axis=-1, keepdims=True)
        expd = jnp.exp(scores - row_peak)
        row_total = jnp.sum(expd, axis=-1, keepdims=True)
        weights_low = (expd / row_total).astype(jnp.bfloat16)
        context = jnp.einsum(
            "hqk,khd->qhd", weights_low, value_heads[:key_end], preferred_element_type=jnp.float32
        )
        pieces.append(context.reshape(block_rows, model_width).astype(jnp.bfloat16))
        log_sums.append(row_peak[..., 0] + jnp.log(row_total[..., 0]))
    return (jnp.concatenate(pieces, axis=0), jnp.concatenate(log_sums, axis=1))


def attend_backward(query_low, key_low, value_low, context_grad, log_sum, causal):
    length, model_width = query_low.shape
    keys_count = key_low.shape[0]
    head_dim = model_width // HEADS
    score_scale = head_dim ** (-0.5)
    block_rows = min(512, length)
    query_heads = query_low.reshape(length, HEADS, head_dim)
    key_heads = key_low.reshape(keys_count, HEADS, head_dim)
    value_heads = value_low.reshape(keys_count, HEADS, head_dim)
    grad_heads = context_grad.reshape(length, HEADS, head_dim)
    key_grads = jnp.zeros((keys_count, HEADS, head_dim), jnp.float32)
    value_grads = jnp.zeros((keys_count, HEADS, head_dim), jnp.float32)
    query_pieces = []
    for row_start in range(0, length, block_rows):
        key_end = row_start + block_rows if causal else keys_count
        query_block = query_heads[row_start : row_start + block_rows]
        grad_block = grad_heads[row_start : row_start + block_rows]
        key_block = key_heads[:key_end]
        scores = block_scores(query_block, key_block, row_start, causal, score_scale)
        probabilities = jnp.exp(scores - log_sum[:, row_start : row_start + block_rows, None])
        weights_low = probabilities.astype(jnp.bfloat16)
        prob_grad = jnp.einsum(
            "qhd,khd->hqk", grad_block, value_heads[:key_end], preferred_element_type=jnp.float32
        )
        row_inner = jnp.sum(prob_grad * probabilities, axis=-1, keepdims=True)
        score_low = (probabilities * (prob_grad - row_inner)).astype(jnp.bfloat16)
        query_pieces.append(
            jnp.einsum("hqk,khd->qhd", score_low, key_block, preferred_element_type=jnp.float32)
            * score_scale
        )
        key_grads = key_grads.at[:key_end].add(
            jnp.einsum("hqk,qhd->khd", score_low, query_block, preferred_element_type=jnp.float32)
            * score_scale
        )
        value_grads = value_grads.at[:key_end].add(
            jnp.einsum("hqk,qhd->khd", weights_low, grad_block, preferred_element_type=jnp.float32)
        )
    query_grad = jnp.concatenate(query_pieces, axis=0).reshape(length, model_width)
    return (
        query_grad.astype(jnp.bfloat16),
        key_grads.reshape(keys_count, model_width).astype(jnp.bfloat16),
        value_grads.reshape(keys_count, model_width).astype(jnp.bfloat16),
    )


def local(
    decoder_in,
    memory,
    cotangent,
    self_query,
    self_query_bias,
    self_key,
    self_value,
    self_value_bias,
    self_output,
    self_output_bias,
    first_gain,
    first_shift,
    cross_query,
    cross_query_bias,
    cross_key,
    cross_value,
    cross_value_bias,
    cross_output,
    cross_output_bias,
    second_gain,
    second_shift,
    expand_weight,
    expand_bias,
    contract_weight,
    contract_bias,
    third_gain,
    third_shift,
):
    gathered = (
        lax.all_gather(self_query, "fsdp", axis=0, tiled=True),
        lax.all_gather(self_query_bias, "fsdp", axis=0, tiled=True),
        lax.all_gather(self_key, "fsdp", axis=0, tiled=True),
        lax.all_gather(self_value, "fsdp", axis=0, tiled=True),
        lax.all_gather(self_value_bias, "fsdp", axis=0, tiled=True),
        lax.all_gather(self_output, "fsdp", axis=0, tiled=True),
        lax.all_gather(self_output_bias, "fsdp", axis=0, tiled=True),
        lax.all_gather(first_gain, "fsdp", axis=0, tiled=True),
        lax.all_gather(first_shift, "fsdp", axis=0, tiled=True),
        lax.all_gather(cross_query, "fsdp", axis=0, tiled=True),
        lax.all_gather(cross_query_bias, "fsdp", axis=0, tiled=True),
        lax.all_gather(cross_key, "fsdp", axis=0, tiled=True),
        lax.all_gather(cross_value, "fsdp", axis=0, tiled=True),
        lax.all_gather(cross_value_bias, "fsdp", axis=0, tiled=True),
        lax.all_gather(cross_output, "fsdp", axis=0, tiled=True),
        lax.all_gather(cross_output_bias, "fsdp", axis=0, tiled=True),
        lax.all_gather(second_gain, "fsdp", axis=0, tiled=True),
        lax.all_gather(second_shift, "fsdp", axis=0, tiled=True),
        lax.all_gather(expand_weight, "fsdp", axis=0, tiled=True),
        lax.all_gather(expand_bias, "fsdp", axis=0, tiled=True),
        lax.all_gather(contract_weight, "fsdp", axis=0, tiled=True),
        lax.all_gather(contract_bias, "fsdp", axis=0, tiled=True),
        lax.all_gather(third_gain, "fsdp", axis=0, tiled=True),
        lax.all_gather(third_shift, "fsdp", axis=0, tiled=True),
    )
    (
        full_sq,
        full_sqb,
        full_sk,
        full_sv,
        full_svb,
        full_so,
        full_sob,
        full_g1,
        full_b1,
        full_cq,
        full_cqb,
        full_ck,
        full_cv,
        full_cvb,
        full_co,
        full_cob,
        full_g2,
        full_b2,
        full_ew,
        full_eb,
        full_cw,
        full_cb,
        full_g3,
        full_b3,
    ) = gathered
    query_low = project(decoder_in, full_sq, full_sqb).astype(jnp.bfloat16)
    key_low = project(decoder_in, full_sk, None).astype(jnp.bfloat16)
    value_low = project(decoder_in, full_sv, full_svb).astype(jnp.bfloat16)
    self_context, self_log_sum = attend_forward(query_low, key_low, value_low, True)
    self_branch = project(self_context, full_so, full_sob)
    first_out, first_normed, first_inv = layer_norm(
        decoder_in.astype(jnp.float32) + self_branch, full_g1, full_b1
    )
    first_low = first_out.astype(jnp.bfloat16)
    cross_q = project(first_low, full_cq, full_cqb).astype(jnp.bfloat16)
    cross_k = project(memory, full_ck, None).astype(jnp.bfloat16)
    cross_v = project(memory, full_cv, full_cvb).astype(jnp.bfloat16)
    cross_context, cross_log_sum = attend_forward(cross_q, cross_k, cross_v, False)
    cross_branch = project(cross_context, full_co, full_cob)
    second_out, second_normed, second_inv = layer_norm(first_out + cross_branch, full_g2, full_b2)
    second_low = second_out.astype(jnp.bfloat16)
    gate_pre = project(second_low, full_ew, full_eb)
    hidden = jax.nn.silu(gate_pre).astype(jnp.bfloat16)
    ffn_branch = project(hidden, full_cw, full_cb)
    final_out, third_normed, third_inv = layer_norm(second_out + ffn_branch, full_g3, full_b3)
    decoder_out = final_out.astype(jnp.bfloat16)
    regathered = (
        lax.all_gather(self_query, "fsdp", axis=0, tiled=True),
        lax.all_gather(self_query_bias, "fsdp", axis=0, tiled=True),
        lax.all_gather(self_key, "fsdp", axis=0, tiled=True),
        lax.all_gather(self_value, "fsdp", axis=0, tiled=True),
        lax.all_gather(self_value_bias, "fsdp", axis=0, tiled=True),
        lax.all_gather(self_output, "fsdp", axis=0, tiled=True),
        lax.all_gather(self_output_bias, "fsdp", axis=0, tiled=True),
        lax.all_gather(first_gain, "fsdp", axis=0, tiled=True),
        lax.all_gather(first_shift, "fsdp", axis=0, tiled=True),
        lax.all_gather(cross_query, "fsdp", axis=0, tiled=True),
        lax.all_gather(cross_query_bias, "fsdp", axis=0, tiled=True),
        lax.all_gather(cross_key, "fsdp", axis=0, tiled=True),
        lax.all_gather(cross_value, "fsdp", axis=0, tiled=True),
        lax.all_gather(cross_value_bias, "fsdp", axis=0, tiled=True),
        lax.all_gather(cross_output, "fsdp", axis=0, tiled=True),
        lax.all_gather(cross_output_bias, "fsdp", axis=0, tiled=True),
        lax.all_gather(second_gain, "fsdp", axis=0, tiled=True),
        lax.all_gather(second_shift, "fsdp", axis=0, tiled=True),
        lax.all_gather(expand_weight, "fsdp", axis=0, tiled=True),
        lax.all_gather(expand_bias, "fsdp", axis=0, tiled=True),
        lax.all_gather(contract_weight, "fsdp", axis=0, tiled=True),
        lax.all_gather(contract_bias, "fsdp", axis=0, tiled=True),
        lax.all_gather(third_gain, "fsdp", axis=0, tiled=True),
        lax.all_gather(third_shift, "fsdp", axis=0, tiled=True),
    )
    (
        full_sq,
        full_sqb,
        full_sk,
        full_sv,
        full_svb,
        full_so,
        full_sob,
        full_g1,
        full_b1,
        full_cq,
        full_cqb,
        full_ck,
        full_cv,
        full_cvb,
        full_co,
        full_cob,
        full_g2,
        full_b2,
        full_ew,
        full_eb,
        full_cw,
        full_cb,
        full_g3,
        full_b3,
    ) = regathered
    g3_grad, b3_grad, third_sum_grad = norm_back(
        cotangent.astype(jnp.float32), third_normed, third_inv, full_g3
    )
    ffn_branch_low = third_sum_grad.astype(jnp.bfloat16)
    cw_grad = weight_grad(hidden, ffn_branch_low)
    cb_grad = column_sum(ffn_branch_low)
    hidden_grad = back_proj(ffn_branch_low, full_cw)
    sigmoid_gate = jax.nn.sigmoid(gate_pre)
    gate_low = (hidden_grad * sigmoid_gate * (1.0 + gate_pre * (1.0 - sigmoid_gate))).astype(
        jnp.bfloat16
    )
    ew_grad = weight_grad(second_low, gate_low)
    eb_grad = column_sum(gate_low)
    second_out_grad = third_sum_grad + back_proj(gate_low, full_ew)
    g2_grad, b2_grad, second_sum_grad = norm_back(
        second_out_grad, second_normed, second_inv, full_g2
    )
    cross_branch_low = second_sum_grad.astype(jnp.bfloat16)
    co_grad = weight_grad(cross_context, cross_branch_low)
    cob_grad = column_sum(cross_branch_low)
    cross_context_low = back_proj(cross_branch_low, full_co).astype(jnp.bfloat16)
    cross_q_low, cross_k_low, cross_v_low = attend_backward(
        cross_q, cross_k, cross_v, cross_context_low, cross_log_sum, False
    )
    cq_grad = weight_grad(first_low, cross_q_low)
    cqb_grad = column_sum(cross_q_low)
    ck_grad = weight_grad(memory, cross_k_low)
    cv_grad = weight_grad(memory, cross_v_low)
    cvb_grad = column_sum(cross_v_low)
    memory_grad = back_proj(cross_k_low, full_ck) + back_proj(cross_v_low, full_cv)
    first_out_grad = second_sum_grad + back_proj(cross_q_low, full_cq)
    g1_grad, b1_grad, first_sum_grad = norm_back(first_out_grad, first_normed, first_inv, full_g1)
    self_branch_low = first_sum_grad.astype(jnp.bfloat16)
    so_grad = weight_grad(self_context, self_branch_low)
    sob_grad = column_sum(self_branch_low)
    self_context_low = back_proj(self_branch_low, full_so).astype(jnp.bfloat16)
    self_q_low, self_k_low, self_v_low = attend_backward(
        query_low, key_low, value_low, self_context_low, self_log_sum, True
    )
    sq_grad = weight_grad(decoder_in, self_q_low)
    sqb_grad = column_sum(self_q_low)
    sk_grad = weight_grad(decoder_in, self_k_low)
    sv_grad = weight_grad(decoder_in, self_v_low)
    svb_grad = column_sum(self_v_low)
    input_grad = (
        first_sum_grad
        + back_proj(self_q_low, full_sq)
        + back_proj(self_k_low, full_sk)
        + back_proj(self_v_low, full_sv)
    )
    shards = (
        lax.psum_scatter(sq_grad, "fsdp", scatter_dimension=0, tiled=True),
        lax.psum_scatter(sqb_grad, "fsdp", scatter_dimension=0, tiled=True),
        lax.psum_scatter(sk_grad, "fsdp", scatter_dimension=0, tiled=True),
        lax.psum_scatter(sv_grad, "fsdp", scatter_dimension=0, tiled=True),
        lax.psum_scatter(svb_grad, "fsdp", scatter_dimension=0, tiled=True),
        lax.psum_scatter(so_grad, "fsdp", scatter_dimension=0, tiled=True),
        lax.psum_scatter(sob_grad, "fsdp", scatter_dimension=0, tiled=True),
        lax.psum_scatter(g1_grad, "fsdp", scatter_dimension=0, tiled=True),
        lax.psum_scatter(b1_grad, "fsdp", scatter_dimension=0, tiled=True),
        lax.psum_scatter(cq_grad, "fsdp", scatter_dimension=0, tiled=True),
        lax.psum_scatter(cqb_grad, "fsdp", scatter_dimension=0, tiled=True),
        lax.psum_scatter(ck_grad, "fsdp", scatter_dimension=0, tiled=True),
        lax.psum_scatter(cv_grad, "fsdp", scatter_dimension=0, tiled=True),
        lax.psum_scatter(cvb_grad, "fsdp", scatter_dimension=0, tiled=True),
        lax.psum_scatter(co_grad, "fsdp", scatter_dimension=0, tiled=True),
        lax.psum_scatter(cob_grad, "fsdp", scatter_dimension=0, tiled=True),
        lax.psum_scatter(g2_grad, "fsdp", scatter_dimension=0, tiled=True),
        lax.psum_scatter(b2_grad, "fsdp", scatter_dimension=0, tiled=True),
        lax.psum_scatter(ew_grad, "fsdp", scatter_dimension=0, tiled=True),
        lax.psum_scatter(eb_grad, "fsdp", scatter_dimension=0, tiled=True),
        lax.psum_scatter(cw_grad, "fsdp", scatter_dimension=0, tiled=True),
        lax.psum_scatter(cb_grad, "fsdp", scatter_dimension=0, tiled=True),
        lax.psum_scatter(g3_grad, "fsdp", scatter_dimension=0, tiled=True),
        lax.psum_scatter(b3_grad, "fsdp", scatter_dimension=0, tiled=True),
    )
    return (
        decoder_out,
        input_grad,
        memory_grad,
        shards[0],
        shards[1],
        shards[2],
        shards[3],
        shards[4],
        shards[5],
        shards[6],
        shards[7],
        shards[8],
        shards[9],
        shards[10],
        shards[11],
        shards[12],
        shards[13],
        shards[14],
        shards[15],
        shards[16],
        shards[17],
        shards[18],
        shards[19],
        shards[20],
        shards[21],
        shards[22],
        shards[23],
    )


def solution(mesh):
    in_specs = (
        P("fsdp", None),
        P("fsdp", None),
        P("fsdp", None),
        P("fsdp", None),
        P("fsdp"),
        P("fsdp", None),
        P("fsdp", None),
        P("fsdp"),
        P("fsdp", None),
        P("fsdp"),
        P("fsdp"),
        P("fsdp"),
        P("fsdp", None),
        P("fsdp"),
        P("fsdp", None),
        P("fsdp", None),
        P("fsdp"),
        P("fsdp", None),
        P("fsdp"),
        P("fsdp"),
        P("fsdp"),
        P("fsdp", None),
        P("fsdp"),
        P("fsdp", None),
        P("fsdp"),
        P("fsdp"),
        P("fsdp"),
    )
    out_specs = (
        P("fsdp", None),
        P("fsdp", None),
        P("fsdp", None),
        P("fsdp", None),
        P("fsdp"),
        P("fsdp", None),
        P("fsdp", None),
        P("fsdp"),
        P("fsdp", None),
        P("fsdp"),
        P("fsdp"),
        P("fsdp"),
        P("fsdp", None),
        P("fsdp"),
        P("fsdp", None),
        P("fsdp", None),
        P("fsdp"),
        P("fsdp", None),
        P("fsdp"),
        P("fsdp"),
        P("fsdp"),
        P("fsdp", None),
        P("fsdp"),
        P("fsdp", None),
        P("fsdp"),
        P("fsdp"),
        P("fsdp"),
    )
    return jax.shard_map(local, mesh=mesh, in_specs=in_specs, out_specs=out_specs, check_vma=False)
```

profile of v0, /device:TPU:0, one launch (start us, length us, event | category | flops | bytes accessed | tf_op | source)
XLA Modules:
  0.0 2020.6 jit_solution(18213995549160198671)
XLA Ops:
  20.8 42.6 %all-reduce.31 = (bf16[512]{0:T(512)(128)(2,1)S(1)}, bf16[512]{0:T(512)(128)(2,1)S(1)}, bf16[512]{0:T(512)(128)(2,1)S(1)}, bf16[512]{0:T(512)(128)(2,1)}, bf16[5...) all-reduce(bf16[512]{0:T(512)(128)(2,1)S(1)} %dynamic-update-slice., ...), channel_id=1, replica_groups=mesh['fsdp'=32] {'fsdp'}, use_global_device_ids=true, to_apply=%add.4 | all-reduce | flops 8704 | bytes 34816
  63.4 43.0 %all_gather.85 = bf16[512,512]{1,0:T(8,128)(2,1)S(1)} all-gather(bf16[16,512]{1,0:T(8,128)(2,1)} %param.85), channel_id=1, replica_groups=mesh['fsdp'=32] {'fsdp'}, dimensions={0}, use_global_device_ids=true | all-gather | bytes 540672 | tf_op jit(solution)/shard_map/all_gather | solution.py:181
  112.7 38.8 %all_gather.89 = bf16[512,512]{1,0:T(8,128)(2,1)S(1)} all-gather(bf16[16,512]{1,0:T(8,128)(2,1)S(1)} %copy-done.117), channel_id=1, replica_groups=mesh['fsdp'=32] {'fsdp'}, dimensions={0}, use_global_device_ids=true | all-gather | bytes 540672 | tf_op jit(solution)/shard_map/all_gather | solution.py:180
  155.4 3.9 copy.89
  162.6 39.4 %all_gather.87 = bf16[512,512]{1,0:T(8,128)(2,1)S(1)} all-gather(bf16[16,512]{1,0:T(8,128)(2,1)S(1)} %copy-done.118), channel_id=1, replica_groups=mesh['fsdp'=32] {'fsdp'}, dimensions={0}, use_global_device_ids=true | all-gather | bytes 540672 | tf_op jit(solution)/shard_map/all_gather | solution.py:178
  202.1 40.7 %all_gather.90 = bf16[512,512]{1,0:T(8,128)(2,1)} all-gather(bf16[16,512]{1,0:T(8,128)(2,1)S(1)} %copy-done.119), channel_id=1, replica_groups=mesh['fsdp'=32] {'fsdp'}, dimensions={0}, use_global_device_ids=true | all-gather | bytes 540672 | tf_op jit(solution)/shard_map/all_gather | solution.py:183
  242.8 42.2 %all_gather.96 = bf16[512,512]{1,0:T(8,128)(2,1)} all-gather(bf16[16,512]{1,0:T(8,128)(2,1)S(1)} %copy-done.120), channel_id=1, replica_groups=mesh['fsdp'=32] {'fsdp'}, dimensions={0}, use_global_device_ids=true | all-gather | bytes 540672 | tf_op jit(solution)/shard_map/all_gather | solution.py:187
  285.0 40.7 %all_gather.98 = bf16[512,512]{1,0:T(8,128)(2,1)} all-gather(bf16[16,512]{1,0:T(8,128)(2,1)S(1)} %copy-done.121), channel_id=1, replica_groups=mesh['fsdp'=32] {'fsdp'}, dimensions={0}, use_global_device_ids=true | all-gather | bytes 540672 | tf_op jit(solution)/shard_map/all_gather | solution.py:189
  325.7 42.3 %all_gather.94 = bf16[512,512]{1,0:T(8,128)(2,1)} all-gather(bf16[16,512]{1,0:T(8,128)(2,1)S(1)} %copy-done.122), channel_id=1, replica_groups=mesh['fsdp'=32] {'fsdp'}, dimensions={0}, use_global_device_ids=true | all-gather | bytes 540672 | tf_op jit(solution)/shard_map/all_gather | solution.py:190
  381.3 3.9 fusion.8
  387.1 5.2 fusion.113
  392.3 10.7 fusion.145
  403.0 11.4 fusion.2
  415.0 11.4 fusion.114
  426.4 13.9 fusion.144
  440.3 13.7 fusion
  454.7 14.6 fusion.115
  507.6 40.7 %all_gather.99 = bf16[512,512]{1,0:T(8,128)(2,1)} all-gather(bf16[16,512]{1,0:T(8,128)(2,1)S(1)} %copy-done.123), channel_id=1, replica_groups=mesh['fsdp'=32] {'fsdp'}, dimensions={0}, use_global_device_ids=true | all-gather | bytes 540672 | tf_op jit(solution)/shard_map/all_gather | solution.py:192
  551.7 4.9 fusion.149
  559.1 14.5 multiply_convert_fusion.4
  573.7 10.9 fusion.150
  587.6 4.2 convert_reduce_fusion.2
  591.8 15.7 convert_reduce_fusion
  607.4 10.6 multiply_reduce_fusion.12
  629.3 4.8 multiply_reduce_fusion.7
  644.5 4.9 multiply_reduce_fusion.6
  649.6 5.4 fusion.94
  655.0 7.5 multiply_reduce_fusion.5
  665.6 4.5 multiply_reduce_fusion.4
  674.9 7.0 multiply_convert_fusion.6
  684.1 4.7 multiply_convert_fusion.7
  689.8 5.1 multiply_convert_fusion.8
  709.7 5.0 fusion.81
  717.3 5.2 fusion.77
  722.5 13.2 fusion.74
  735.8 15.6 convert_reduce_fusion.6
  751.4 4.8 convolution_add_fusion.5
  756.2 3.7 convolution_add_fusion.4
  764.5 5.1 multiply_reduce_fusion.3
  774.1 6.8 multiply_convert_fusion.5
  787.5 5.2 fusion.118
  792.8 24.1 %multiply_reduce_fusion = (f32[8,512]{1,0:T(8,128)S(1)}, f32[8,512,2048]{2,1,0:T(8,128)}) fusion(f32[8,512,2048]{2,1,0:T(8,128)} %get-tuple-element.421, f32[8,512]{1,0:T(8,128)S(1)} %copy-done.94, bf16[512,8,64]{0,2,1:T(8,128)(2,1)} %bitcast.313, bf16[2048,8,64]{0,2,1:T(8,128)(2,1)S(1)} %bitcast.283), kind=kOutput, calls=%fused_computation.1 | convolution fusion | flops 1098903552 | bytes 69763072 | tf_op jit(solution)/shard_map/qhd,khd->hqk/dot_general | solution.py:124
  817.1 28.1 %multiply_convert_fusion = bf16[8,512,2048]{2,1,0:T(8,128)(2,1)} fusion(f32[8,512,2048]{2,1,0:T(8,128)} %get-tuple-element.461, f32[8,512,2048]{2,1,0:T(8,128)} %get-tuple-element.421, f32[8,512]{1,0:T(8,128)S(1)} %get-tuple-element.460, f32[8,512]{1,0:T(8,128)S(1)} %copy-done.94), kind=kLoop, calls=%fused_computation | loop fusion | flops 33554432 | bytes 83918848 | tf_op jit(solution)/shard_map/convert_element_type | solution.py:128
  845.2 11.8 fusion.86
  857.0 11.6 multiply_reduce_fusion.2
  868.7 12.1 multiply_convert_fusion.2
  886.8 15.6 multiply_reduce_fusion.1
  902.5 22.9 %multiply_convert_fusion.1 = bf16[8,512,1536]{2,1,0:T(8,128)(2,1)} fusion(f32[8,512,1536]{2,1,0:T(8,128)} %get-tuple-element.459, f32[8,512,1536]{2,1,0:T(8,128)} %get-tuple-element.423, f32[8,512]{1,0:T(8,128)S(1)} %get-tuple-element.458, f32[8,512]{1,0:T(8,128)S(1)} %copy-done.98), kind=kLoop, calls=%fused_computation.8 | loop fusion | flops 25165824 | bytes 62947328 | tf_op jit(solution)/shard_map/convert_element_type | solution.py:128
  929.2 8.6 fusion.92
  942.5 6.9 fusion.78
  949.8 9.4 fusion.65
  959.1 10.2 fusion.46
  974.2 10.5 fusion.154
  985.4 11.3 fusion.135
  997.4 3.9 copy.117
  1001.7 37.9 %all-reduce.30 = (f32[512]{0:T(512)S(1)}, f32[512]{0:T(512)S(1)}, f32[512]{0:T(512)S(1)}, f32[512]{0:T(512)S(1)}, f32[512]{0:T(512)S(1)}, /*index=5*/f32[512]{0:...) all-reduce(f32[512]{0:T(512)S(1)} %reduce_sum.415, ...), channel_id=3, replica_groups=mesh['fsdp'=32] {'fsdp'}, use_global_device_ids=true, to_apply=%region_38.39.clone | all-reduce | flops 8704 | bytes 69632
  1054.8 5.5 copy.118
  1062.9 126.6 %reduce-scatter.21.cloned.1.call-done = f32[16,512]{1,0:T(8,128)} async-done(((f32[512,512]{1,0:T(8,128)}), f32[16,512]{1,0:T(8,128)}) %reduce-scatter.21.cloned.1.call-update) | async-done | bytes 32784 | tf_op jit(solution)/shard_map/reduce_scatter | solution.py:358
  1189.5 135.2 %reduce-scatter.37.cloned.1.call-done = f32[16,512]{1,0:T(8,128)} async-done(((f32[512,512]{1,0:T(8,128)}), f32[16,512]{1,0:T(8,128)}) %reduce-scatter.37.cloned.1.call-update) | async-done | bytes 32784
  1324.7 135.4 %reduce-scatter.35.cloned.1.call-done = f32[16,512]{1,0:T(8,128)} async-done(((f32[512,512]{1,0:T(8,128)}), f32[16,512]{1,0:T(8,128)}) %reduce-scatter.35.cloned.1.call-update) | async-done | bytes 32784
  1460.2 135.3 %reduce-scatter.31.cloned.1.call-done = f32[16,512]{1,0:T(8,128)} async-done(((f32[512,512]{1,0:T(8,128)}), f32[16,512]{1,0:T(8,128)}) %reduce-scatter.31.cloned.1.call-update) | async-done | bytes 32784
  1595.4 135.1 %reduce-scatter.33.cloned.1.call-done = f32[16,512]{1,0:T(8,128)} async-done(((f32[512,512]{1,0:T(8,128)}), f32[16,512]{1,0:T(8,128)}) %reduce-scatter.33.cloned.1.call-update) | async-done | bytes 32784
  1730.5 141.6 %reduce-scatter.29.cloned.1.call-done = f32[64,512]{1,0:T(8,128)} async-done(((f32[2048,512]{1,0:T(8,128)}), f32[64,512]{1,0:T(8,128)}) %reduce-scatter.29.cloned.1.call-update) | async-done | bytes 131088 | tf_op jit(solution)/shard_map/reduce_scatter | solution.py:373
  1872.1 141.2 %reduce-scatter.27.cloned.1.call-done = f32[16,2048]{1,0:T(8,128)} async-done(((f32[512,2048]{1,0:T(8,128)}), f32[16,2048]{1,0:T(8,128)}) %reduce-scatter.27.cloned.1.call-update) | async-done | bytes 131088 | tf_op jit(solution)/shard_map/reduce_scatter | solution.py:371
  (545 shorter events, 194.7 us)
Async XLA Ops:
  7.2 469.3 %copy-start = (bf16[512,512]{1,0:T(8,128)(2,1)S(1)}, bf16[512,512]{1,0:T(8,128)(2,1)}, u32[]{:S(2)}) copy-start(bf16[512,512]{1,0:T(8,128)(2,1)} %param.80) | copy-start | bytes 1572868
  7.2 551.9 %all-gather.3.cloned.1.call-start = ((), (), s32[]{:S(2)}) async-start(), calls=%async_computation.10 | async-start | bytes 2162688 | tf_op jit(solution)/shard_map/all_gather | solution.py:196
  8.0 565.7 %all-gather.5.cloned.1.call-start = ((), (), s32[]{:S(2)}) async-start(), calls=%async_computation.11 | async-start | bytes 2162688 | tf_op jit(solution)/shard_map/all_gather | solution.py:198
  8.7 1054.2 %reduce-scatter.25.cloned.1.call-start = ((), (), s32[]{:S(2)}) async-start(), calls=%async_computation.14 | async-start | bytes 1081344 | tf_op jit(solution)/shard_map/reduce_scatter | solution.py:367
  109.5 43.4 %copy-start.28 = (bf16[2048,512]{0,1:T(8,128)(2,1)}, bf16[2048,512]{0,1:T(8,128)(2,1)S(1)}, u32[]{:S(2)}) copy-start(bf16[2048,512]{0,1:T(8,128)(2,1)S(1)} %add_convert_fusion.3) | copy-start | bytes 6291460
  109.5 42.0 %copy-start.80 = (bf16[2048,512]{1,0:T(8,128)(2,1)S(1)}, bf16[2048,512]{1,0:T(8,128)(2,1)}, u32[]{:S(2)}) copy-start(bf16[2048,512]{1,0:T(8,128)(2,1)} %param.79) | copy-start | bytes 6291460
  152.8 273.6 %copy-start.18 = (bf16[2048,512]{0,1:T(8,128)(2,1)}, bf16[2048,512]{0,1:T(8,128)(2,1)S(1)}, u32[]{:S(2)}) copy-start(bf16[2048,512]{0,1:T(8,128)(2,1)S(1)} %convolution_convert_fusion.2) | copy-start | bytes 6291460
  152.9 217.8 %copy-start.48 = (bf16[512,512]{0,1:T(8,128)(2,1)}, bf16[512,512]{0,1:T(8,128)(2,1)S(1)}, u32[]{:S(2)}) copy-start(bf16[512,512]{0,1:T(8,128)(2,1)S(1)} %slice.524) | copy-start | bytes 1572868
  154.1 47.9 %copy-start.119 = (bf16[16,512]{1,0:T(8,128)(2,1)S(1)}, bf16[16,512]{1,0:T(8,128)(2,1)}, u32[]{:S(2)}) copy-start(bf16[16,512]{1,0:T(8,128)(2,1)} %param.87) | copy-start | bytes 49156
  154.1 88.7 %copy-start.120 = (bf16[16,512]{1,0:T(8,128)(2,1)S(1)}, bf16[16,512]{1,0:T(8,128)(2,1)}, u32[]{:S(2)}) copy-start(bf16[16,512]{1,0:T(8,128)(2,1)} %param.91) | copy-start | bytes 49156
  154.1 130.9 %copy-start.121 = (bf16[16,512]{1,0:T(8,128)(2,1)S(1)}, bf16[16,512]{1,0:T(8,128)(2,1)}, u32[]{:S(2)}) copy-start(bf16[16,512]{1,0:T(8,128)(2,1)} %param.93) | copy-start | bytes 49156
  155.4 170.2 %copy-start.122 = (bf16[16,512]{1,0:T(8,128)(2,1)S(1)}, bf16[16,512]{1,0:T(8,128)(2,1)}, u32[]{:S(2)}) copy-start(bf16[16,512]{1,0:T(8,128)(2,1)} %param.94) | copy-start | bytes 49156
  159.3 209.8 %copy-start.81 = (bf16[2048,512]{1,0:T(8,128)(2,1)S(1)}, bf16[2048,512]{1,0:T(8,128)(2,1)}, u32[]{:S(2)}) copy-start(bf16[2048,512]{1,0:T(8,128)(2,1)} %param.79) | copy-start | bytes 6291460
  202.1 167.1 %copy-start.92 = (bf16[512,512]{1,0:T(8,128)(2,1)}, bf16[512,512]{1,0:T(8,128)(2,1)S(1)}, u32[]{:S(2)}) copy-start(bf16[512,512]{1,0:T(8,128)(2,1)S(1)} %all_gather.87) | copy-start | bytes 1572868
  370.7 21.7 %copy-start.39 = (bf16[512,512]{0,1:T(8,128)(2,1)}, bf16[512,512]{0,1:T(8,128)(2,1)S(1)}, u32[]{:S(2)}) copy-start(bf16[512,512]{0,1:T(8,128)(2,1)S(1)} %get-tuple-element.418) | copy-start | bytes 1572868
  370.7 55.7 %copy-start.41 = (bf16[512,512]{0,1:T(8,128)(2,1)}, bf16[512,512]{0,1:T(8,128)(2,1)S(1)}, u32[]{:S(2)}) copy-start(bf16[512,512]{0,1:T(8,128)(2,1)S(1)} %get-tuple-element.417) | copy-start | bytes 1572868
  403.0 12.0 copy-start.43
  440.3 14.3 copy-start.29
  454.6 14.6 copy-start.95
  454.7 14.6 copy-start.141
  473.0 78.6 %copy-start.104 = (f32[2048]{0:T(1024)}, f32[2048]{0:T(1024)S(1)}, u32[]{:S(2)}) copy-start(f32[2048]{0:T(1024)S(1)} %broadcast_multiply_fusion.8) | copy-start | bytes 24580
  473.8 77.9 %copy-start.106 = (f32[2048]{0:T(1024)}, f32[2048]{0:T(1024)S(1)}, u32[]{:S(2)}) copy-start(f32[2048]{0:T(1024)S(1)} %add_rsqrt_fusion.2) | copy-start | bytes 24580
  477.4 15.3 copy-start.64
  477.4 22.7 %copy-start.66 = (bf16[512,512]{0,1:T(8,128)(2,1)}, bf16[512,512]{0,1:T(8,128)(2,1)S(1)}, u32[]{:S(2)}) copy-start(bf16[512,512]{0,1:T(8,128)(2,1)S(1)} %get-tuple-element.415) | copy-start | bytes 1572868
  477.9 22.2 %copy-start.10 = (bf16[512,512]{0,1:T(8,128)(2,1)}, bf16[512,512]{0,1:T(8,128)(2,1)S(1)}, u32[]{:S(2)}) copy-start(bf16[512,512]{0,1:T(8,128)(2,1)S(1)} %convolution_convert_fusion.3) | copy-start | bytes 1572868
  507.4 110.6 %copy-start.130 = (f32[512]{0:T(512)}, f32[512]{0:T(512)S(1)}, u32[]{:S(2)}) copy-start(f32[512]{0:T(512)S(1)} %convert_element_type.355) | copy-start | bytes 6148
  507.5 66.2 %copy-start.138 = (f32[512]{0:T(512)}, f32[512]{0:T(512)S(1)}, u32[]{:S(2)}) copy-start(f32[512]{0:T(512)S(1)} %convert_element_type.356) | copy-start | bytes 6148
  556.6 61.5 %copy-start.108 = (f32[2048]{0:T(1024)}, f32[2048]{0:T(1024)S(1)}, u32[]{:S(2)}) copy-start(f32[2048]{0:T(1024)S(1)} %broadcast_multiply_fusion.7) | copy-start | bytes 24580
  559.1 59.0 %copy-start.112 = (f32[2048]{0:T(1024)}, f32[2048]{0:T(1024)S(1)}, u32[]{:S(2)}) copy-start(f32[2048]{0:T(1024)S(1)} %add_rsqrt_fusion.1) | copy-start | bytes 24580
  591.8 15.7 copy-start.87
  591.8 15.7 copy-start.27
  624.5 9.7 slice-start.16
  629.3 12.7 slice-start.12
  649.5 413.4 %reduce-scatter.39.cloned.1.call-start = ((), (), s32[]{:S(2)}) async-start(), calls=%async_computation.21 | async-start | bytes 1081344
  649.5 12.9 slice-start.8
  654.9 10.6 slice-start.6
  654.9 8.8 slice-start.9
  654.9 10.6 slice-start.7
  674.9 9.0 slice-start.10
  674.9 9.2 slice-start.11
  703.9 13.4 slice-start
  703.9 13.4 slice-start.1
  705.9 11.4 slice-start.2
  722.5 13.2 copy-start.94
  751.4 10.8 copy-start.33
  751.4 8.6 copy-start.13
  769.6 293.3 %reduce-scatter.23.cloned.1.call-start = ((), (), s32[]{:S(2)}) async-start(), calls=%async_computation.13 | async-start | bytes 1081344 | tf_op jit(solution)/shard_map/reduce_scatter | solution.py:362
  774.1 8.8 copy-start.63
  792.8 396.7 %reduce-scatter.21.cloned.1.call-start = ((), (), s32[]{:S(2)}) async-start(), calls=%async_computation.12 | async-start | bytes 1081344 | tf_op jit(solution)/shard_map/reduce_scatter | solution.py:358
  817.0 507.7 %reduce-scatter.37.cloned.1.call-start = ((), (), s32[]{:S(2)}) async-start(), calls=%async_computation.20 | async-start | bytes 1081344
  817.1 28.1 %copy-start.19 = (bf16[2048,512]{0,1:T(8,128)(2,1)S(1)}, bf16[2048,512]{0,1:T(8,128)(2,1)}, u32[]{:S(2)}) copy-start(bf16[2048,512]{0,1:T(8,128)(2,1)} %copy-done.18) | copy-start | bytes 6291460
  868.6 591.5 %reduce-scatter.35.cloned.1.call-start = ((), (), s32[]{:S(2)}) async-start(), calls=%async_computation.19 | async-start | bytes 1081344
  868.7 15.4 copy-start.32
  902.4 693.0 %reduce-scatter.31.cloned.1.call-start = ((), (), s32[]{:S(2)}) async-start(), calls=%async_computation.17 | async-start | bytes 1081344
  902.5 22.9 %copy-start.15 = (bf16[8,512,512]{1,2,0:T(8,128)(2,1)S(1)}, bf16[8,512,512]{1,2,0:T(8,128)(2,1)}, u32[]{:S(2)}) copy-start(bf16[8,512,512]{1,2,0:T(8,128)(2,1)} %copy-done.14) | copy-start | bytes 12582916
  902.5 22.9 %copy-start.49 = (bf16[512,512]{0,1:T(8,128)(2,1)S(1)}, bf16[512,512]{0,1:T(8,128)(2,1)}, u32[]{:S(2)}) copy-start(bf16[512,512]{0,1:T(8,128)(2,1)} %copy-done.48) | copy-start | bytes 1572868
  949.5 9.6 copy-start.42
  949.5 781.0 %reduce-scatter.33.cloned.1.call-start = ((), (), s32[]{:S(2)}) async-start(), calls=%async_computation.18 | async-start | bytes 1081344
  959.1 10.2 copy-start.84
  974.1 897.9 %reduce-scatter.29.cloned.1.call-start = ((), (), s32[]{:S(2)}) async-start(), calls=%async_computation.16 | async-start | bytes 4325376 | tf_op jit(solution)/shard_map/reduce_scatter | solution.py:373
  984.7 1028.6 %reduce-scatter.27.cloned.1.call-start = ((), (), s32[]{:S(2)}) async-start(), calls=%async_computation.15 | async-start | bytes 4325376 | tf_op jit(solution)/shard_map/reduce_scatter | solution.py:371
  996.8 50.4 %copy-start.91 = (bf16[512,512]{1,0:T(8,128)(2,1)S(1)}, bf16[512,512]{1,0:T(8,128)(2,1)}, u32[]{:S(2)}) copy-start(bf16[512,512]{1,0:T(8,128)(2,1)} %copy-done.90) | copy-start | bytes 1572868
  1039.5 8.9 copy-start.36
  1039.6 8.9 copy-start.93
  (120 other events, 456.5 us)
Sparse Core Ops, SparseCore 0:
  10.9 59.1 all-gather.2
  73.0 55.5 all-gather.4
  649.6 134.0 reduce-scatter.24
  786.4 132.5 reduce-scatter.38
  921.6 132.5 reduce-scatter.22
  1056.9 132.4 reduce-scatter.20
  1192.3 132.3 reduce-scatter.36
  1327.5 132.5 reduce-scatter.34
  1463.0 132.3 reduce-scatter.30
  1598.1 132.3 reduce-scatter.32
  1733.4 138.6 reduce-scatter.28
  1874.8 138.4 reduce-scatter.26
where the time goes:
time: 2030 us; the launch traced here: 2020 us
  waiting for transfers between devices  952 us (47%)
  blocking collectives  408 us (20%)
  matrix products  402 us (20%)
  other arithmetic  151 us (7%)
  local copies, waits for them, and re-layouts  89.9 us (4%)
    unnamed x17, waiting for transfers between devices  543 us
    reduce_scatter x1, waiting for transfers between devices, local(): lax.psum_scatter(cw_grad, 'fsdp', scatter_dimension=0, tiled=True)  142 us
    reduce_scatter x1, waiting for transfers between devices, local(): lax.psum_scatter(ew_grad, 'fsdp', scatter_dimension=0, tiled=True)  141 us
    reduce_scatter x1, waiting for transfers between devices, local(): lax.psum_scatter(so_grad, 'fsdp', scatter_dimension=0, tiled=True)  127 us
    convert_element_type x8, other arithmetic, attend_backward(): score_low = (probabilities * (prob_grad - row_inner)).astype(jnp.bfloat16)  89.3 us
    unnamed x2, blocking collectives  80.5 us
    dot_general x8, matrix products, attend_backward(): jnp.einsum('qhd,khd->hqk', grad_block, value_heads[:key_end], preferred_e...  78.2 us
    unnamed x395, local copies, waits for them, and re-layouts  76.3 us
  transfers between devices with their start and end apart: 12, of which 7 were waited for; matrix products, arithmetic and copies ran while one was open for 27% of the time, Pallas kernels for 0%

commit v1 on v0

v1 whole, which is shorter than its diff:
```python
import functools

import jax
import jax.numpy as jnp
from jax import lax
from jax.experimental import pallas as pl
from jax.experimental.pallas import tpu as pltpu
from jax.sharding import PartitionSpec as P

HEADS = 8
EPS = 1e-05
BF = jnp.bfloat16
F32 = jnp.float32
QB = 256
ROWS = 256

VECS = (
    "sqb", "svb", "sob", "g1", "b1", "cqb", "cvb", "cob", "g2", "b2", "cb", "g3", "b3",
)
EB_ROW = len(VECS)
ROW_OF = {name: row for row, name in enumerate(VECS)}


def dot_nn(a, b):
    return lax.dot_general(a, b, (((1,), (0,)), ((), ())), preferred_element_type=F32)


def dot_nt(a, b):
    return lax.dot_general(a, b, (((1,), (1,)), ((), ())), preferred_element_type=F32)


def dot_tn(a, b):
    return lax.dot_general(a, b, (((0,), (0,)), ((), ())), preferred_element_type=F32)


def stage_sizes(n):
    sizes = []
    while n > 4:
        sizes.append(2)
        n //= 2
    return (n, *sizes)


def strides_of(sizes):
    strides, stride = [], 1
    for size in reversed(sizes):
        strides.append(stride)
        stride *= size
    return tuple(reversed(strides))


def shift_perm(n, stride, size, by):
    pairs = []
    for source in range(n):
        digit = (source // stride) % size
        pairs.append((source, source + ((digit + by) % size - digit) * stride))
    return pairs


def gather_rows(block, n):
    sizes = stage_sizes(n)
    strides = strides_of(sizes)
    index = lax.axis_index("fsdp")
    size, stride = sizes[0], strides[0]
    digit = (index // stride) % size
    pieces = [block]
    for by in range(1, size):
        pieces.append(lax.ppermute(block, "fsdp", shift_perm(n, stride, size, by)))
    table = jnp.stack([pieces[(size - 1 - t) % size] for t in range(2 * size - 1)])
    whole = lax.dynamic_slice_in_dim(table, size - 1 - digit, size, 0)
    for size, stride in zip(sizes[1:], strides[1:]):
        digit = (index // stride) % size
        other = lax.ppermute(whole, "fsdp", shift_perm(n, stride, size, 1))
        first = jnp.where(digit == 0, whole, other)
        second = jnp.where(digit == 0, other, whole)
        whole = jnp.stack([first, second], axis=1)
        whole = whole.reshape((-1,) + block.shape)
    return whole


def scatter_rows(partial, n):
    sizes = stage_sizes(n)
    strides = strides_of(sizes)
    index = lax.axis_index("fsdp")
    rest = partial
    for size, stride in reversed(list(zip(sizes[1:], strides[1:]))):
        digit = (index // stride) % size
        pairs = rest.reshape((-1, 2) + rest.shape[1:])
        send = lax.dynamic_index_in_dim(pairs, 1 - digit, 1, False)
        keep = lax.dynamic_index_in_dim(pairs, digit, 1, False)
        got = lax.ppermute(send, "fsdp", shift_perm(n, stride, size, 1))
        rest = (keep.astype(F32) + got.astype(F32)).astype(BF)
    size, stride = sizes[0], strides[0]
    digit = (index // stride) % size
    total = lax.dynamic_index_in_dim(rest, digit, 0, False).astype(F32)
    for by in range(1, size):
        send = lax.dynamic_index_in_dim(rest, (digit + by) % size, 0, False)
        got = lax.ppermute(send, "fsdp", shift_perm(n, stride, size, by))
        total = total + got.astype(F32)
    return total


def pair_masks(rows):
    lane = lax.broadcasted_iota(jnp.int32, (rows, 128), 1)
    return lane < 64


def self_forward_kernel(q_ref, k_ref, v_ref, o_ref, lse_ref):
    length = q_ref.shape[0]
    keys = k_ref[...]
    vt = v_ref[...].T
    top = lax.broadcasted_iota(jnp.int32, vt.shape, 0) < 64
    ones = jnp.ones_like(vt)
    vt_heads = (jnp.where(top, vt, ones), jnp.where(top, ones, vt))
    first_half = pair_masks(QB)
    keep = lax.broadcasted_iota(jnp.int32, (QB, QB), 0) <= lax.broadcasted_iota(
        jnp.int32, (QB, QB), 1
    )
    for start in range(0, length, QB):
        end = start + QB
        query = q_ref[start:end, :] * jnp.asarray(0.125, BF)
        zeros = jnp.zeros_like(query)
        parts, logs = [], []
        for head in range(2):
            own = jnp.where(first_half if head == 0 else ~first_half, query, zeros)
            last = jnp.where(keep, dot_nt(keys[start:end], own), -1e30)
            peak = jnp.max(last, axis=0, keepdims=True)
            if start:
                scores = dot_nt(keys[:start], own)
                peak = jnp.maximum(peak, jnp.max(scores, axis=0, keepdims=True))
            expd = jnp.exp(last - peak).astype(BF)
            acc = dot_nn(vt_heads[head][:, start:end], expd)
            if start:
                expd = jnp.exp(scores - peak).astype(BF)
                acc = acc + dot_nn(vt_heads[head][:, :start], expd)
            if head == 0:
                total = acc[64:65]
                parts.append(acc[:64] / total)
            else:
                total = acc[:1]
                parts.append(acc[64:] / total)
            logs.append(peak + jnp.log(total))
        context = jnp.concatenate(parts, axis=0)
        o_ref[start:end, :] = context.T.astype(BF)
        lse_ref[0, :, start:end] = jnp.concatenate(logs, axis=0)


def self_forward(query, key, value):
    length, width = query.shape
    pairs = width // 128
    spec = pl.BlockSpec((length, 128), lambda p: (0, p))
    area = length * length // 2
    return pl.pallas_call(
        self_forward_kernel,
        grid=(pairs,),
        in_specs=[spec, spec, spec],
        out_specs=[spec, pl.BlockSpec((1, 2, length), lambda p: (p, 0, 0))],
        out_shape=[
            jax.ShapeDtypeStruct((length, width), BF),
            jax.ShapeDtypeStruct((pairs, 2, length), F32),
        ],
        cost_estimate=pl.CostEstimate(
            flops=4 * area * width * 4, bytes_accessed=8 * length * width,
            transcendentals=area * HEADS,
        ),
        name="self_forward",
    )(query, key, value)


def self_backward_kernel(
    q_ref, k_ref, v_ref, o_ref, g_ref, lse_ref, dq_ref, dk_ref, dv_ref, dk_acc, dv_acc
):
    length = q_ref.shape[0]
    keys = k_ref[...]
    values = v_ref[...]
    kt = keys.T
    first_half = pair_masks(QB)
    top = lax.broadcasted_iota(jnp.int32, (128, QB), 0) < 64
    keep = lax.broadcasted_iota(jnp.int32, (QB, QB), 0) <= lax.broadcasted_iota(
        jnp.int32, (QB, QB), 1
    )
    for start in range(0, length, QB):
        end = start + QB
        query = q_ref[start:end, :] * jnp.asarray(0.125, BF)
        grad = g_ref[start:end, :]
        inner = (grad.astype(F32) * o_ref[start:end, :].astype(F32)).T
        zeros = jnp.zeros_like(query)
        weights_of, scores_of, own_q, own_g, dq_parts = [], [], [], [], []
        for head in range(2):
            mine = first_half if head == 0 else ~first_half
            own = jnp.where(mine, query, zeros)
            own_grad = jnp.where(mine, grad, zeros)
            delta = jnp.sum(inner[head * 64 : head * 64 + 64], axis=0, keepdims=True)
            log_sum = lse_ref[0, head : head + 1, start:end]
            scores = dot_nt(keys[:end], own)
            if start:
                scores = jnp.concatenate(
                    [scores[:start], jnp.where(keep, scores[start:], -1e30)], axis=0
                )
            else:
                scores = jnp.where(keep, scores, -1e30)
            probs = jnp.exp(scores - log_sum)
            prob_grad = dot_nt(values[:end], own_grad)
            score_low = (probs * (prob_grad - delta)).astype(BF)
            dq_parts.append(dot_nn(kt[:, :end], score_low))
            weights_of.append(probs.astype(BF))
            scores_of.append(score_low)
            own_q.append(own)
            own_g.append(own_grad)
        dq = jnp.where(top, dq_parts[0], dq_parts[1]) * 0.125
        dq_ref[start:end, :] = dq.T.astype(BF)
        dk = dot_nn(scores_of[0], own_q[0]) + dot_nn(scores_of[1], own_q[1])
        dv = dot_nn(weights_of[0], own_g[0]) + dot_nn(weights_of[1], own_g[1])
        if start:
            dk_acc[:start, :] += dk[:start]
            dv_acc[:start, :] += dv[:start]
        dk_acc[start:end, :] = dk[start:]
        dv_acc[start:end, :] = dv[start:]
    dk_ref[...] = dk_acc[...].astype(BF)
    dv_ref[...] = dv_acc[...].astype(BF)


def self_backward(query, key, value, context, grad, log_sum):
    length, width = query.shape
    pairs = width // 128
    spec = pl.BlockSpec((length, 128), lambda p: (0, p))
    area = length * length // 2
    shape = jax.ShapeDtypeStruct((length, width), BF)
    return pl.pallas_call(
        self_backward_kernel,
        grid=(pairs,),
        in_specs=[spec] * 5 + [pl.BlockSpec((1, 2, length), lambda p: (p, 0, 0))],
        out_specs=[spec, spec, spec],
        out_shape=[shape, shape, shape],
        scratch_shapes=[pltpu.VMEM((length, 128), F32), pltpu.VMEM((length, 128), F32)],
        cost_estimate=pl.CostEstimate(
            flops=10 * area * width * 4, bytes_accessed=16 * length * width,
            transcendentals=area * HEADS,
        ),
        name="self_backward",
    )(query, key, value, context, grad, log_sum)


def norm(summed, gain, shift):
    mean = jnp.mean(summed, axis=-1, keepdims=True)
    centred = summed - mean
    inverse = lax.rsqrt(jnp.mean(centred * centred, axis=-1, keepdims=True) + EPS)
    normed = centred * inverse
    return normed * gain + shift, normed, inverse


def norm_back(incoming, normed, inverse, gain):
    scaled = incoming * gain
    return inverse * (
        scaled
        - jnp.mean(scaled, axis=-1, keepdims=True)
        - normed * jnp.mean(scaled * normed, axis=-1, keepdims=True)
    )


def col_sum(value):
    return jnp.sum(value.astype(F32), axis=0, keepdims=True)


def middle_kernel(
    x_ref, ctx_ref, cot_ref, k_ref, v_ref, so_ref, cq_ref, co_ref, ew_ref, cw_ref, vec_ref,
    out_ref, fsg_ref, scl_ref,
    dso_ref, dcq_ref, dco_ref, dew_ref, dcw_ref, dk_ref, dv_ref, dvec_ref,
    expd_ref,
):
    step = pl.program_id(0)
    width = x_ref.shape[1]
    inner = ew_ref.shape[1]
    pairs = width // 128
    rows = x_ref.shape[0]

    @pl.when(step == 0)
    def _():
        for ref in (dso_ref, dcq_ref, dco_ref, dew_ref, dcw_ref, dk_ref, dv_ref, dvec_ref):
            ref[...] = jnp.zeros_like(ref)

    def vec(name):
        row = ROW_OF[name]
        return vec_ref[row : row + 1, :]

    def add_vec(name, value):
        row = ROW_OF[name]
        dvec_ref[row : row + 1, :] += value

    context = ctx_ref[...]
    branch = dot_nn(context, so_ref[...]) + vec("sob")
    first_out, first_normed, first_inv = norm(
        x_ref[...].astype(F32) + branch, vec("g1"), vec("b1")
    )
    first_low = first_out.astype(BF)
    cross_q = (dot_nn(first_low, cq_ref[...]) + vec("cqb")).astype(BF)
    scaled_q = cross_q * jnp.asarray(0.125, BF)
    first_half = pair_masks(rows)
    zeros = jnp.zeros((rows, 128), BF)
    keys_count = k_ref.shape[0]
    top = lax.broadcasted_iota(jnp.int32, (128, keys_count), 0) < 64
    ones = jnp.ones((128, keys_count), BF)
    own_q, totals, contexts = [], [], []
    for pair in range(pairs):
        at = slice(pair * 128, pair * 128 + 128)
        key = k_ref[:, at]
        vt = v_ref[:, at].T
        parts = []
        for head in range(2):
            mine = first_half if head == 0 else ~first_half
            own = jnp.where(mine, scaled_q[:, at], zeros)
            scores = dot_nt(key, own)
            peak = jnp.max(scores, axis=0, keepdims=True)
            expd = jnp.exp(scores - peak).astype(BF)
            expd_ref[pair * 2 + head] = expd
            if head == 0:
                acc = dot_nn(jnp.where(top, vt, ones), expd)
                total = 1.0 / acc[64:65]
                parts.append(acc[:64] * total)
            else:
                acc = dot_nn(jnp.where(top, ones, vt), expd)
                total = 1.0 / acc[:1]
                parts.append(acc[64:] * total)
            own_q.append(own)
            totals.append(total)
        contexts.append(jnp.concatenate(parts, axis=0))
    context_t = jnp.concatenate(contexts, axis=0)
    cross_context = context_t.T.astype(BF)
    second_out, second_normed, second_inv = norm(
        first_out + dot_nn(cross_context, co_ref[...]) + vec("cob"), vec("g2"), vec("b2")
    )
    second_low = second_out.astype(BF)
    gate_bias = jnp.concatenate(
        [vec_ref[EB_ROW + j : EB_ROW + j + 1, :] for j in range(inner // width)], axis=1
    )
    gate_pre = dot_nn(second_low, ew_ref[...]) + gate_bias
    sig = 1.0 / (1.0 + jnp.exp(-gate_pre))
    silu = gate_pre * sig
    hidden = silu.astype(BF)
    slope = sig + silu * (1.0 - sig)
    final_out, third_normed, third_inv = norm(
        second_out + dot_nn(hidden, cw_ref[...]) + vec("cb"), vec("g3"), vec("b3")
    )
    out_ref[...] = final_out.astype(BF)

    incoming = cot_ref[...].astype(F32)
    add_vec("g3", col_sum(incoming * third_normed))
    add_vec("b3", col_sum(incoming))
    third_sum = norm_back(incoming, third_normed, third_inv, vec("g3"))
    branch_low = third_sum.astype(BF)
    dcw_ref[...] += dot_tn(hidden, branch_low)
    add_vec("cb", col_sum(branch_low))
    gate_low = (dot_nt(branch_low, cw_ref[...]) * slope).astype(BF)
    dew_ref[...] += dot_tn(second_low, gate_low)
    gate_sum = col_sum(gate_low)
    for j in range(inner // width):
        dvec_ref[EB_ROW + j : EB_ROW + j + 1, :] += gate_sum[:, j * width : (j + 1) * width]
    second_grad = third_sum + dot_nt(gate_low, ew_ref[...])
    add_vec("g2", col_sum(second_grad * second_normed))
    add_vec("b2", col_sum(second_grad))
    second_sum = norm_back(second_grad, second_normed, second_inv, vec("g2"))
    cross_low = second_sum.astype(BF)
    dco_ref[...] += dot_tn(cross_context, cross_low)
    add_vec("cob", col_sum(cross_low))
    grad_t = dot_nt(co_ref[...], cross_low)
    inner_t = grad_t * context_t
    dq_parts = []
    for pair in range(pairs):
        at = slice(pair * 128, pair * 128 + 128)
        key = k_ref[:, at]
        kt = key.T
        value = v_ref[:, at]
        scaled = jnp.concatenate(
            [
                grad_t[pair * 128 : pair * 128 + 64] * totals[pair * 2],
                grad_t[pair * 128 + 64 : pair * 128 + 128] * totals[pair * 2 + 1],
            ],
            axis=0,
        )
        grad = scaled.T.astype(BF)
        key_grad, value_grad, query_grad = [], [], []
        for head in range(2):
            mine = first_half if head == 0 else ~first_half
            own_grad = jnp.where(mine, grad, zeros)
            low = pair * 128 + head * 64
            delta = jnp.sum(inner_t[low : low + 64], axis=0, keepdims=True) * totals[
                pair * 2 + head
            ]
            expd = expd_ref[pair * 2 + head]
            score_low = (expd.astype(F32) * (dot_nt(value, own_grad) - delta)).astype(BF)
            query_grad.append(dot_nn(kt, score_low))
            key_grad.append(dot_nn(score_low, own_q[pair * 2 + head]))
            value_grad.append(dot_nn(expd, own_grad))
        dk_ref[:, at] += key_grad[0] + key_grad[1]
        dv_ref[:, at] += value_grad[0] + value_grad[1]
        dq_parts.append(query_grad[0][:64])
        dq_parts.append(query_grad[1][64:])
    cross_q_low = (jnp.concatenate(dq_parts, axis=0) * 0.125).T.astype(BF)
    dcq_ref[...] += dot_tn(first_low, cross_q_low)
    add_vec("cqb", col_sum(cross_q_low))
    first_grad = second_sum + dot_nt(cross_q_low, cq_ref[...])
    add_vec("g1", col_sum(first_grad * first_normed))
    add_vec("b1", col_sum(first_grad))
    first_sum = norm_back(first_grad, first_normed, first_inv, vec("g1"))
    fsg_ref[...] = first_sum
    self_low = first_sum.astype(BF)
    dso_ref[...] += dot_tn(context, self_low)
    add_vec("sob", col_sum(self_low))
    scl_ref[...] = dot_nt(self_low, so_ref[...]).astype(BF)


def middle(x, context, cotangent, cross_k, cross_v, so, cq, co, ew, cw, vecs):
    length, width = x.shape
    inner = ew.shape[1]
    block = pl.BlockSpec((ROWS, width), lambda i: (i, 0))

    def fixed(array):
        return pl.BlockSpec(array.shape, lambda i: (0,) * len(array.shape))

    square = jax.ShapeDtypeStruct((width, width), F32)
    mem = jax.ShapeDtypeStruct(cross_k.shape, F32)
    outs = [
        jax.ShapeDtypeStruct((length, width), BF),
        jax.ShapeDtypeStruct((length, width), F32),
        jax.ShapeDtypeStruct((length, width), BF),
        square, square, square,
        jax.ShapeDtypeStruct((width, inner), F32),
        jax.ShapeDtypeStruct((inner, width), F32),
        mem, mem,
        jax.ShapeDtypeStruct(vecs.shape, F32),
    ]
    weights = (cross_k, cross_v, so, cq, co, ew, cw, vecs)
    return pl.pallas_call(
        middle_kernel,
        grid=(length // ROWS,),
        in_specs=[block] * 3 + [
            pl.BlockSpec(w.shape, lambda i: (0, 0), pipeline_mode=pl.Buffered(1))
            for w in weights
        ],
        out_specs=[block] * 3 + [
            pl.BlockSpec(o.shape, lambda i: (0, 0), pipeline_mode=pl.Buffered(1))
            for o in outs[3:]
        ],
        out_shape=outs,
        scratch_shapes=[pltpu.VMEM((HEADS, cross_k.shape[0], ROWS), BF)],
        cost_estimate=pl.CostEstimate(
            flops=12 * length * width * inner + 60 * length * width * width,
            bytes_accessed=60 << 20,
            transcendentals=length * inner * 2 + length * cross_k.shape[0] * HEADS,
        ),
        name="middle",
    )(x, context, cotangent, *weights)


def local(n, *args):
    (
        decoder_in, memory, cotangent,
        self_query, self_query_bias, self_key, self_value, self_value_bias,
        self_output, self_output_bias, first_gain, first_shift,
        cross_query, cross_query_bias, cross_key, cross_value, cross_value_bias,
        cross_output, cross_output_bias, second_gain, second_shift,
        expand_weight, expand_bias, contract_weight, contract_bias,
        third_gain, third_shift,
    ) = args
    width = decoder_in.shape[1]
    small = self_query_bias.shape[0]
    rows = self_query.shape[0]
    inner = expand_weight.shape[1]
    wide = inner // width
    vectors = (
        self_query_bias, self_value_bias, self_output_bias, first_gain, first_shift,
        cross_query_bias, cross_value_bias, cross_output_bias, second_gain, second_shift,
        contract_bias, third_gain, third_shift,
    )
    count = len(vectors)
    packed = jnp.concatenate(vectors + (expand_bias,))
    pad = jnp.zeros((rows * width - packed.shape[0],), BF)
    packed = jnp.concatenate([packed, pad]).reshape(rows, width)

    got_self = gather_rows(
        jnp.concatenate([self_query, self_key, self_value, packed], axis=0), n
    )

    def whole(gathered, at, size):
        return gathered[:, at : at + size].reshape(n * size, width)

    full_sq = whole(got_self, 0, rows)
    full_sk = whole(got_self, rows, rows)
    full_sv = whole(got_self, 2 * rows, rows)
    flat = got_self[:, 3 * rows :].reshape(n, rows * width)
    table = flat[:, : count * small].reshape(n, count, small).transpose(1, 0, 2)
    table = table.reshape(count, width)
    gate_bias = flat[:, count * small : (count + wide) * small].reshape(wide, width)
    fill = jnp.zeros((-(count + wide) % 8, width), BF)
    vecs = jnp.concatenate([table, gate_bias, fill], axis=0).astype(F32)

    got_cross = gather_rows(
        jnp.concatenate(
            [self_output, cross_query, cross_key, cross_value, cross_output], axis=0
        ),
        n,
    )
    got_ffn = gather_rows(
        jnp.concatenate(
            [expand_weight[:, j * width : (j + 1) * width] for j in range(wide)]
            + [contract_weight],
            axis=0,
        ),
        n,
    )
    full_so, full_cq, full_ck, full_cv, full_co = [
        whole(got_cross, j * rows, rows) for j in range(5)
    ]
    full_ew = jnp.concatenate([whole(got_ffn, j * rows, rows) for j in range(wide)], axis=1)
    full_cw = whole(got_ffn, wide * rows, contract_weight.shape[0])

    query = (dot_nn(decoder_in, full_sq) + vecs[ROW_OF["sqb"]]).astype(BF)
    key = dot_nn(decoder_in, full_sk).astype(BF)
    value = (dot_nn(decoder_in, full_sv) + vecs[ROW_OF["svb"]]).astype(BF)
    context, log_sum = self_forward(query, key, value)
    cross_k = dot_nn(memory, full_ck).astype(BF)
    cross_v = (dot_nn(memory, full_cv) + vecs[ROW_OF["cvb"]]).astype(BF)
    (
        decoder_out, first_sum, context_low, dso, dcq, dco, dew, dcw, dck, dcv, dvec,
    ) = middle(
        decoder_in, context, cotangent, cross_k, cross_v,
        full_so, full_cq, full_co, full_ew, full_cw, vecs,
    )
    cross_k_low = dck.astype(BF)
    cross_v_low = dcv.astype(BF)
    memory_grad = dot_nt(cross_k_low, full_ck) + dot_nt(cross_v_low, full_cv)
    ck_grad = dot_tn(memory, cross_k_low)
    cv_grad = dot_tn(memory, cross_v_low)
    cvb_grad = jnp.sum(cross_v_low.astype(F32), axis=0)

    def split(grad):
        return grad.astype(BF).reshape(n, -1, width)

    def split_vec(rows_of):
        stacked = jnp.stack(rows_of).reshape(len(rows_of), n, small).transpose(1, 0, 2)
        flat = stacked.reshape(n, -1).astype(BF)
        pad = jnp.zeros((n, rows * width - flat.shape[1]), BF)
        return jnp.concatenate([flat, pad], axis=1).reshape(n, rows, width)

    names = ("sob", "g1", "b1", "cqb", "cob", "g2", "b2", "cb", "g3", "b3")
    vec_rows = [dvec[ROW_OF[name]] for name in names] + [cvb_grad]
    gate_flat = dvec[EB_ROW : EB_ROW + wide].reshape(n, wide * small)
    flat = jnp.stack(vec_rows).reshape(len(vec_rows), n, small).transpose(1, 0, 2)
    flat = jnp.concatenate([flat.reshape(n, -1), gate_flat], axis=1).astype(BF)
    vec_pad = jnp.zeros((n, rows * width - flat.shape[1]), BF)
    vec_block = jnp.concatenate([flat, vec_pad], axis=1).reshape(n, rows, width)
    mid = jnp.concatenate(
        [split(g) for g in (dso, dcq, ck_grad, cv_grad, dco)]
        + [split(dew[:, j * width : (j + 1) * width]) for j in range(wide)]
        + [split(dcw), vec_block],
        axis=1,
    )
    mid_sum = scatter_rows(mid, n)

    self_q_low, self_k_low, self_v_low = self_backward(
        query, key, value, context, context_low, log_sum
    )
    sq_grad = dot_tn(decoder_in, self_q_low)
    sk_grad = dot_tn(decoder_in, self_k_low)
    sv_grad = dot_tn(decoder_in, self_v_low)
    sqb_grad = jnp.sum(self_q_low.astype(F32), axis=0)
    svb_grad = jnp.sum(self_v_low.astype(F32), axis=0)
    last = jnp.concatenate(
        [split(g) for g in (sq_grad, sk_grad, sv_grad)] + [split_vec([sqb_grad, svb_grad])],
        axis=1,
    )
    last_sum = scatter_rows(last, n)
    input_grad = (
        first_sum
        + dot_nt(self_q_low, full_sq)
        + dot_nt(self_k_low, full_sk)
        + dot_nt(self_v_low, full_sv)
    )

    def take(total, at, size):
        return total[at : at + size]

    so_out, cq_out, ck_out, cv_out, co_out = [take(mid_sum, j * rows, rows) for j in range(5)]
    ew_out = jnp.concatenate(
        [take(mid_sum, (5 + j) * rows, rows) for j in range(wide)], axis=1
    )
    at = (5 + wide) * rows
    cw_out = take(mid_sum, at, contract_weight.shape[0])
    flat = mid_sum[at + contract_weight.shape[0] :].reshape(-1)
    vec_out = {
        name: flat[j * small : (j + 1) * small] for j, name in enumerate(names + ("cvb",))
    }
    at = (len(names) + 1) * small
    eb_out = flat[at : at + wide * small]
    flat = last_sum[3 * rows :].reshape(-1)
    sq_out, sk_out, sv_out = [take(last_sum, j * rows, rows) for j in range(3)]
    return (
        decoder_out, input_grad, memory_grad,
        sq_out, flat[:small], sk_out, sv_out, flat[small : 2 * small],
        so_out, vec_out["sob"], vec_out["g1"], vec_out["b1"],
        cq_out, vec_out["cqb"], ck_out, cv_out, vec_out["cvb"],
        co_out, vec_out["cob"], vec_out["g2"], vec_out["b2"],
        ew_out, eb_out, cw_out, vec_out["cb"], vec_out["g3"], vec_out["b3"],
    )


MATRICES = (0, 1, 2, 3, 5, 6, 8, 12, 14, 15, 17, 21, 23)


def solution(mesh):
    n = mesh.shape["fsdp"]
    specs = tuple(P("fsdp", None) if j in MATRICES else P("fsdp") for j in range(27))
    return jax.shard_map(
        functools.partial(local, n), mesh=mesh, in_specs=specs, out_specs=specs, check_vma=False
    )
```

time: 2030 us -> 494 us (0.24)
  waiting for transfers between devices: 952 us -> 127 us
  blocking collectives: 408 us -> 0 us
  matrix products: 402 us -> 30.6 us
  Pallas kernels: 0 us -> 215 us
  other arithmetic: 151 us -> 23.4 us
  local copies, waits for them, and re-layouts: 89.9 us -> 53.9 us
  starting transfers between devices: 0.96 us -> 34.8 us
    unnamed x17 -> x0, waiting for transfers between devices: 543 us -> none
    reduce_scatter x5 -> x0, waiting for transfers between devices: 409 us -> none  [the longest x1 142 us: local(): lax.psum_scatter(cw_grad, 'fsdp', scatter_dimension=0, tiled=True)]
    dot_general x78 -> x15, matrix products: 402 us -> 30.6 us  [the longest x5 12.2 us: dot_nn(): lax.dot_general(a, b, (((1,), (0,)), ((), ())), preferred_element_type=F32)]
    all_gather x8 -> x0, blocking collectives: 328 us -> none  [the longest x1 43 us: local(): lax.all_gather(self_value, 'fsdp', axis=0, tiled=True)]
    pallas_call x0 -> x3, Pallas kernels: none -> 215 us  [the longest x1 116 us: middle(): pl.pallas_call(middle_kernel, grid=(length // ROWS,), in_specs=[block] *...]
    ppermute x0 -> x30, waiting for transfers between devices: none -> 127 us  [the longest x6 60.2 us: scatter_rows(): got = lax.ppermute(send, 'fsdp', shift_perm(n, stride, size, 1))]
    convert_element_type x23 -> x12, other arithmetic: 92.9 us -> 8.11 us  [the longest x6 5.97 us: scatter_rows(): rest = (keep.astype(F32) + got.astype(F32)).astype(BF)]
    unnamed x2 -> x0, blocking collectives: 80.5 us -> none
  transfers between devices with their start and end apart: 12 -> 30, of which waited for: 7 -> 13; matrix products, arithmetic and copies ran while one was open for 27% -> 12% of each run, Pallas kernels for 0% -> 20%
where the time goes in v1:
time: 494 us; the launch traced here: 486 us
  Pallas kernels  215 us (44%)
  waiting for transfers between devices  127 us (26%)
  local copies, waits for them, and re-layouts  53.9 us (11%)
  starting transfers between devices  34.8 us (7%)
  matrix products  30.6 us (6%)
  other arithmetic  23.4 us (5%)
    pallas_call x1, Pallas kernels, middle(): pl.pallas_call(middle_kernel, grid=(length // ROWS,), in_specs=[block] *...  116 us
    ppermute x6, waiting for transfers between devices, scatter_rows(): got = lax.ppermute(send, 'fsdp', shift_perm(n, stride, size, 1))  60.2 us
    pallas_call x1, Pallas kernels, self_backward(): pl.pallas_call(self_backward_kernel, grid=(pairs,), in_specs=[spec] * 5 +...  53.4 us
    pallas_call x1, Pallas kernels, self_forward(): pl.pallas_call(self_forward_kernel, grid=(pairs,), in_specs=[spec, spec,...  44.9 us
    ppermute x9, waiting for transfers between devices, gather_rows(): other = lax.ppermute(whole, 'fsdp', shift_perm(n, stride, size, 1))  40.8 us
    unnamed x118, local copies, waits for them, and re-layouts  23.2 us
    ppermute x6, waiting for transfers between devices, scatter_rows(): got = lax.ppermute(send, 'fsdp', shift_perm(n, stride, size, by))  18.2 us
    ppermute x9, starting transfers between devices, gather_rows(): pieces.append(lax.ppermute(block, 'fsdp', shift_perm(n, stride, size, by)))  14.6 us
  transfers between devices with their start and end apart: 30, of which 13 were waited for; matrix products, arithmetic and copies ran while one was open for 12% of the time, Pallas kernels for 20%

profile of v1, /device:TPU:0, one launch (start us, length us, event | category | flops | bytes accessed | tf_op | source)
XLA Modules:
  0.0 486.5 jit_solution(15871076799865623037)
XLA Ops:
  1.5 9.4 %concatenate.73 = bf16[8192]{0:T(1024)(128)(2,1)S(1)} concatenate(bf16[16]{0:T(256)(128)(2,1)} %param.31, bf16[16]{0:T(256)(128)(2,1)} %param.34, bf16[16]{0:T(256)(128)(2,1)} %param.36, bf16[16]{0:T(256)(128)(2,1)} %param.37, bf16[16]{0:T(256)(128)(2,1)} %param.38, bf16[16]{0:T(256)(128)(2,1)} %param.40, bf16[16]{0:T(256)(128)(2,1)} %param.43, bf16[16]{0:T(256)(128)(2,1)} %param.45, ...), dimensions={0} | concatenate | bytes 32768 | tf_op jit(solution)/shard_map/concatenate | solution.py:478
  12.4 5.1 %collective-permute-start = (bf16[64,512]{1,0:T(8,128)(2,1)S(1)}, bf16[64,512]{1,0:T(8,128)(2,1)S(1)}, u32[]{:S(2)}, u32[]{:S(2)}) collective-permute-start(bf16[64,512]{1,0:T(8,128)(2,1)S(1)} %constant_dynamic-update-slice_fusion), channel_id=1, source_target_pairs={{0,24},{1,25},{2,26},{3,27},{4,28},{5,29},{6,30},{7,31},{8,0},{9,1... | collective-permute-start | bytes 196616 | tf_op jit(solution)/shard_map/ppermute | solution.py:68
  17.5 1.0 collective-permute-start.2
  22.1 2.8 collective-permute-start.6
  24.9 1.1 collective-permute-start.7
  29.8 3.9 collective-permute-start.12
  34.5 1.6 collective-permute-start.3
  37.0 1.6 collective-permute-start.9
  38.6 6.9 %collective-permute-done.13 = bf16[128,512]{1,0:T(8,128)(2,1)S(1)} collective-permute-done((bf16[128,512]{1,0:T(8,128)(2,1)S(1)}, bf16[128,512]{1,0:T(8,128)(2,1)S(1)}, u32[]{:S(2)}, u32[]{:S(2)}) %collective-permute-start.13) | collective-permute-done | bytes 131104 | tf_op jit(solution)/shard_map/ppermute | solution.py:68
  45.7 1.6 collective-permute-start.15
  47.4 1.6 collective-permute-start.4
  49.7 8.9 %collective-permute-done.15 = bf16[4,128,512]{2,1,0:T(8,128)(2,1)S(1)} collective-permute-done((bf16[4,128,512]{2,1,0:T(8,128)(2,1)S(1)}, bf16[4,128,512]{2,1,0:T(8,128)(2,1)S(1)}, u32[]{:S(2)}, u32[]{:S(2)}) %collective-permute-start.15) | collective-permute-done | bytes 524320 | tf_op jit(solution)/shard_map/ppermute | solution.py:73
  58.8 1.6 collective-permute-start.16
  60.3 2.0 collective-permute-done.4
  62.4 1.1 select_bitcast_fusion.13
  63.6 1.1 copy.147
  64.8 11.6 %collective-permute-done.10 = bf16[8,80,512]{2,1,0:T(8,128)(2,1)S(1)} collective-permute-done((bf16[8,80,512]{2,1,0:T(8,128)(2,1)S(1)}, bf16[8,80,512]{2,1,0:T(8,128)(2,1)S(1)}, u32[]{:S(2)}, u32[]{:S(2)}) %collective-permute-start.10) | collective-permute-done | bytes 655392 | tf_op jit(solution)/shard_map/ppermute | solution.py:73
  76.6 1.1 copy.155
  77.7 18.3 %collective-permute-done.16 = bf16[8,128,512]{2,1,0:T(8,128)(2,1)} collective-permute-done((bf16[8,128,512]{2,1,0:T(8,128)(2,1)S(1)}, bf16[8,128,512]{2,1,0:T(8,128)(2,1)}, u32[]{:S(2)}, u32[]{:S(2)}) %collective-permute-start.16) | collective-permute-done | bytes 1048608 | tf_op jit(solution)/shard_map/ppermute | solution.py:73
  96.1 1.4 select_bitcast_fusion.5
  97.9 1.7 select_bitcast_fusion.7
  100.0 1.2 fusion.27
  102.2 4.4 fusion.4.k_ref
  106.6 2.6 fusion.2.q_ref
  109.2 2.7 fusion.3.v_ref
  111.9 44.9 %self_forward.1 = (bf16[2048,512]{1,0:T(8,128)(2,1)}, f32[4,2,2048]{2,1,0:T(2,128)}) custom-call(bf16[2048,512]{1,0:T(8,128)(2,1)} %fusion.2.q_ref, bf16[2048,512]{1,0:T(8,128)(2,1)} %fusion.4.k_ref, bf16[2048,512]{1,0:T(8,128)(2,1)} %fusion.3.v_ref), custom_call_target="tpu_custom_call" | custom-call | flops 17179869184 | bytes 8388608 | tf_op jit(solution)/shard_map/self_forward/pallas_call | solution.py:153
  156.8 1.9 select_bitcast_fusion.3
  159.2 1.2 fusion.25
  160.4 1.2 fusion.9.k_ref
  161.6 1.3 fusion.8.v_ref
  162.9 1.9 select_bitcast_fusion.1
  165.8 1.5 slice.271
  167.3 1.6 pad_maximum_fusion.4.ew_ref
  169.0 116.4 %middle.1 = (bf16[2048,512]{1,0:T(8,128)(2,1)}, f32[2048,512]{1,0:T(8,128)}, bf16[2048,512]{1,0:T(8,128)(2,1)}, f32[512,512]{1,0:T(8,128)}, f32[512,512]{1,0:T(8...) custom-call(bf16[2048,512]{1,0:T(8,128)(2,1)} %x_ref.1, ...), custom_call_target="tpu_custom_call" | custom-call | flops 57982058496 | bytes 62914560 | tf_op jit(solution)/shard_map/middle/pallas_call | solution.py:433
  285.4 2.7 convolution_convert_fusion.2
  290.2 1.3 convolution_convert_fusion.3
  292.7 1.3 fusion.26
  294.0 1.6 copy-done.9
  296.7 2.1 constant_dynamic-update-slice_fusion.37
  304.9 1.5 constant_dynamic-update-slice_fusion.29
  307.3 4.2 dynamic-slice_bitcast_fusion
  312.0 53.4 %self_backward.1 = (bf16[2048,512]{1,0:T(8,128)(2,1)}, bf16[2048,512]{1,0:T(8,128)(2,1)}, bf16[2048,512]{1,0:T(8,128)(2,1)}) custom-call(bf16[2048,512]{1,0:T(8,128)(2,1)} %fusion.2.q_ref, bf16[2048,512]{1,0:T(8,128)(2,1)} %fusion.4.k_ref, bf16[2048,512]{1,0:T(8,128)(2,1)} %fusion.3.v_ref, bf16[2048,512]{1,0:T(8,128)(2,1)} %get-tuple-element.43.ctx_ref.o_ref, ...), custom_call_target="tpu_custom_call" | custom-call | flops 42949672960 | bytes 16777216 | tf_op jit(solution)/shard_map/self_backward/pallas_call | solution.py:229
  365.4 2.1 reduce.1
  368.5 3.7 convolution_convert_fusion.4
  372.2 1.3 convolution_convert_fusion.6
  373.8 1.3 convolution_convert_fusion.5
  376.5 1.3 fusion.35
  378.4 3.2 fusion
  381.8 1.6 collective-permute-start.25
  383.4 1.3 fusion.34
  384.8 1.7 fusion.5
  387.4 3.7 add_add_fusion
  391.2 43.9 %collective-permute-done.19 = bf16[8,64,512]{2,1,0:T(8,128)(2,1)S(1)} collective-permute-done((bf16[8,64,512]{2,1,0:T(8,128)(2,1)S(1)}, bf16[8,64,512]{2,1,0:T(8,128)(2,1)S(1)}, u32[]{:S(2)}, u32[]{:S(2)}) %collective-permute-start.19) | collective-permute-done | bytes 524320 | tf_op jit(solution)/shard_map/ppermute | solution.py:91
  436.5 1.6 collective-permute-start.26
  438.6 5.9 %collective-permute-done.20 = bf16[4,64,512]{2,1,0:T(8,128)(2,1)S(1)} collective-permute-done((bf16[4,64,512]{2,1,0:T(8,128)(2,1)S(1)}, bf16[4,64,512]{2,1,0:T(8,128)(2,1)S(1)}, u32[]{:S(2)}, u32[]{:S(2)}) %collective-permute-start.20) | collective-permute-done | bytes 262176 | tf_op jit(solution)/shard_map/ppermute | solution.py:91
  444.7 1.3 collective-permute-start.22
  445.9 1.9 collective-permute-start.21
  447.9 1.4 convolution_add_fusion.1
  449.9 2.1 collective-permute-done.21
  452.0 10.3 %collective-permute-done.26 = bf16[4,224,512]{2,1,0:T(8,128)(2,1)S(1)} collective-permute-done((bf16[4,224,512]{2,1,0:T(8,128)(2,1)S(1)}, bf16[4,224,512]{2,1,0:T(8,128)(2,1)S(1)}, u32[]{:S(2)}, u32[]{:S(2)}) %collective-permute-start.26) | collective-permute-done | bytes 917536 | tf_op jit(solution)/shard_map/ppermute | solution.py:91
  462.7 1.3 collective-permute-start.28
  464.0 1.9 collective-permute-start.27
  467.2 2.6 collective-permute-done.29
  469.8 12.9 %collective-permute-done.28 = bf16[224,512]{1,0:T(8,128)(2,1)S(1)} collective-permute-done((bf16[224,512]{1,0:T(8,128)(2,1)S(1)}, bf16[224,512]{1,0:T(8,128)(2,1)S(1)}, u32[]{:S(2)}, u32[]{:S(2)}) %collective-permute-start.28) | collective-permute-done | bytes 229408 | tf_op jit(solution)/shard_map/ppermute | solution.py:98
  (233 shorter events, 39.9 us)
Async XLA Ops:
  0.7 159.7 %copy-start = (bf16[512,512]{1,0:T(8,128)(2,1)S(1)}, bf16[512,512]{1,0:T(8,128)(2,1)}, u32[]{:S(2)}) copy-start(bf16[512,512]{1,0:T(8,128)(2,1)} %param.28) | copy-start | bytes 1572868
  12.4 17.3 %collective-permute-start = (bf16[64,512]{1,0:T(8,128)(2,1)S(1)}, bf16[64,512]{1,0:T(8,128)(2,1)S(1)}, u32[]{:S(2)}, u32[]{:S(2)}) collective-permute-start(bf16[64,512]{1,0:T(8,128)(2,1)S(1)} %constant_dynamic-update-slice_fusion), channel_id=1, source_target_pairs={{0,24},{1,25},{2,26},{3,27},{4,28},{5,29},{6,30},{7,31},{8,0},{9,1... | collective-permute-start | bytes 196616 | tf_op jit(solution)/shard_map/ppermute | solution.py:68
  17.5 12.3 %collective-permute-start.1 = (bf16[64,512]{1,0:T(8,128)(2,1)S(1)}, bf16[64,512]{1,0:T(8,128)(2,1)S(1)}, u32[]{:S(2)}, u32[]{:S(2)}) collective-permute-start(bf16[64,512]{1,0:T(8,128)(2,1)S(1)} %constant_dynamic-update-slice_fusion), channel_id=1, source_target_pairs={{0,16},{1,17},{2,18},{3,19},{4,20},{5,21},{6,22},{7,23},{8,24},{9,... | collective-permute-start | bytes 196616 | tf_op jit(solution)/shard_map/ppermute | solution.py:68
  17.5 16.2 %collective-permute-start.2 = (bf16[64,512]{1,0:T(8,128)(2,1)S(1)}, bf16[64,512]{1,0:T(8,128)(2,1)S(1)}, u32[]{:S(2)}, u32[]{:S(2)}) collective-permute-start(bf16[64,512]{1,0:T(8,128)(2,1)S(1)} %constant_dynamic-update-slice_fusion), channel_id=1, source_target_pairs={{0,8},{1,9},{2,10},{3,11},{4,12},{5,13},{6,14},{7,15},{8,16},{9,17... | collective-permute-start | bytes 196616 | tf_op jit(solution)/shard_map/ppermute | solution.py:68
  22.1 11.8 %collective-permute-start.6 = (bf16[80,512]{1,0:T(8,128)(2,1)S(1)}, bf16[80,512]{1,0:T(8,128)(2,1)S(1)}, u32[]{:S(2)}, u32[]{:S(2)}) collective-permute-start(bf16[80,512]{1,0:T(8,128)(2,1)S(1)} %constant_dynamic-update-slice_fusion.11), channel_id=1, source_target_pairs={{0,24},{1,25},{2,26},{3,27},{4,28},{5,29},{6,30},{7,31},{8,0},{9,1... | collective-permute-start | bytes 245768 | tf_op jit(solution)/shard_map/ppermute | solution.py:68
  24.9 9.6 %collective-permute-start.7 = (bf16[80,512]{1,0:T(8,128)(2,1)S(1)}, bf16[80,512]{1,0:T(8,128)(2,1)S(1)}, u32[]{:S(2)}, u32[]{:S(2)}) collective-permute-start(bf16[80,512]{1,0:T(8,128)(2,1)S(1)} %constant_dynamic-update-slice_fusion.11), channel_id=1, source_target_pairs={{0,16},{1,17},{2,18},{3,19},{4,20},{5,21},{6,22},{7,23},{8,24},{9,... | collective-permute-start | bytes 245768 | tf_op jit(solution)/shard_map/ppermute | solution.py:68
  29.7 7.2 %collective-permute-start.8 = (bf16[80,512]{1,0:T(8,128)(2,1)S(1)}, bf16[80,512]{1,0:T(8,128)(2,1)S(1)}, u32[]{:S(2)}, u32[]{:S(2)}) collective-permute-start(bf16[80,512]{1,0:T(8,128)(2,1)S(1)} %constant_dynamic-update-slice_fusion.11), channel_id=1, source_target_pairs={{0,8},{1,9},{2,10},{3,11},{4,12},{5,13},{6,14},{7,15},{8,16},{9,17... | collective-permute-start | bytes 245768 | tf_op jit(solution)/shard_map/ppermute | solution.py:68
  29.8 8.9 %collective-permute-start.12 = (bf16[128,512]{1,0:T(8,128)(2,1)S(1)}, bf16[128,512]{1,0:T(8,128)(2,1)S(1)}, u32[]{:S(2)}, u32[]{:S(2)}) collective-permute-start(bf16[128,512]{1,0:T(8,128)(2,1)S(1)} %constant_dynamic-update-slice_fusion.23), channel_id=1, source_target_pairs={{0,24},{1,25},{2,26},{3,27},{4,28},{5,29},{6,30},{7,31},{8,0},{9,1... | collective-permute-start | bytes 393224 | tf_op jit(solution)/shard_map/ppermute | solution.py:68
  33.6 11.9 %collective-permute-start.13 = (bf16[128,512]{1,0:T(8,128)(2,1)S(1)}, bf16[128,512]{1,0:T(8,128)(2,1)S(1)}, u32[]{:S(2)}, u32[]{:S(2)}) collective-permute-start(bf16[128,512]{1,0:T(8,128)(2,1)S(1)} %constant_dynamic-update-slice_fusion.23), channel_id=1, source_target_pairs={{0,16},{1,17},{2,18},{3,19},{4,20},{5,21},{6,22},{7,23},{8,24},{9,... | collective-permute-start | bytes 393224 | tf_op jit(solution)/shard_map/ppermute | solution.py:68
  33.8 11.7 %collective-permute-start.14 = (bf16[128,512]{1,0:T(8,128)(2,1)S(1)}, bf16[128,512]{1,0:T(8,128)(2,1)S(1)}, u32[]{:S(2)}, u32[]{:S(2)}) collective-permute-start(bf16[128,512]{1,0:T(8,128)(2,1)S(1)} %constant_dynamic-update-slice_fusion.23), channel_id=1, source_target_pairs={{0,8},{1,9},{2,10},{3,11},{4,12},{5,13},{6,14},{7,15},{8,16},{9,17... | collective-permute-start | bytes 393224 | tf_op jit(solution)/shard_map/ppermute | solution.py:68
  34.5 12.8 %collective-permute-start.3 = (bf16[4,64,512]{2,1,0:T(8,128)(2,1)S(1)}, bf16[4,64,512]{2,1,0:T(8,128)(2,1)S(1)}, u32[]{:S(2)}, u32[]{:S(2)}) collective-permute-start(bf16[4,64,512]{2,1,0:T(8,128)(2,1)S(1)} %constant_dynamic-slice_fusion.2), channel_id=1, source_target_pairs={{0,4},{1,5},{2,6},{3,7},{4,0},{5,1},{6,2},{7,3},{8,12},{9,13},{10,... | collective-permute-start | bytes 786440 | tf_op jit(solution)/shard_map/ppermute | solution.py:73
  37.0 11.9 %collective-permute-start.9 = (bf16[4,80,512]{2,1,0:T(8,128)(2,1)S(1)}, bf16[4,80,512]{2,1,0:T(8,128)(2,1)S(1)}, u32[]{:S(2)}, u32[]{:S(2)}) collective-permute-start(bf16[4,80,512]{2,1,0:T(8,128)(2,1)S(1)} %constant_dynamic-slice_fusion.1), channel_id=1, source_target_pairs={{0,4},{1,5},{2,6},{3,7},{4,0},{5,1},{6,2},{7,3},{8,12},{9,13},{10,... | collective-permute-start | bytes 983048 | tf_op jit(solution)/shard_map/ppermute | solution.py:73
  45.7 12.9 %collective-permute-start.15 = (bf16[4,128,512]{2,1,0:T(8,128)(2,1)S(1)}, bf16[4,128,512]{2,1,0:T(8,128)(2,1)S(1)}, u32[]{:S(2)}, u32[]{:S(2)}) collective-permute-start(bf16[4,128,512]{2,1,0:T(8,128)(2,1)S(1)} %constant_dynamic-slice_fusion), channel_id=1, source_target_pairs={{0,4},{1,5},{2,6},{3,7},{4,0},{5,1},{6,2},{7,3},{8,12},{9,13},{10,... | collective-permute-start | bytes 1572872 | tf_op jit(solution)/shard_map/ppermute | solution.py:73
  47.4 15.0 %collective-permute-start.4 = (bf16[8,64,512]{2,1,0:T(8,128)(2,1)S(1)}, bf16[8,64,512]{2,1,0:T(8,128)(2,1)}, u32[]{:S(2)}, u32[]{:S(2)}) collective-permute-start(bf16[8,64,512]{2,1,0:T(8,128)(2,1)S(1)} %bitcast.270), channel_id=1, source_target_pairs={{0,2},{1,3},{2,0},{3,1},{4,6},{5,7},{6,4},{7,5},{8,10},{9,11},{10,... | collective-permute-start | bytes 1572872 | tf_op jit(solution)/shard_map/ppermute | solution.py:73
  49.1 27.2 %collective-permute-start.10 = (bf16[8,80,512]{2,1,0:T(8,128)(2,1)S(1)}, bf16[8,80,512]{2,1,0:T(8,128)(2,1)S(1)}, u32[]{:S(2)}, u32[]{:S(2)}) collective-permute-start(bf16[8,80,512]{2,1,0:T(8,128)(2,1)S(1)} %bitcast.267), channel_id=1, source_target_pairs={{0,2},{1,3},{2,0},{3,1},{4,6},{5,7},{6,4},{7,5},{8,10},{9,11},{10,... | collective-permute-start | bytes 1966088 | tf_op jit(solution)/shard_map/ppermute | solution.py:73
  58.8 37.3 %collective-permute-start.16 = (bf16[8,128,512]{2,1,0:T(8,128)(2,1)S(1)}, bf16[8,128,512]{2,1,0:T(8,128)(2,1)}, u32[]{:S(2)}, u32[]{:S(2)}) collective-permute-start(bf16[8,128,512]{2,1,0:T(8,128)(2,1)S(1)} %bitcast.264), channel_id=1, source_target_pairs={{0,2},{1,3},{2,0},{3,1},{4,6},{5,7},{6,4},{7,5},{8,10},{9,11},{10,... | collective-permute-start | bytes 3145736 | tf_op jit(solution)/shard_map/ppermute | solution.py:73
  64.7 33.2 %collective-permute-start.5 = (bf16[16,64,512]{2,1,0:T(8,128)(2,1)}, bf16[16,64,512]{2,1,0:T(8,128)(2,1)}, u32[]{:S(2)}, u32[]{:S(2)}) collective-permute-start(bf16[16,64,512]{2,1,0:T(8,128)(2,1)} %bitcast.10), channel_id=1, source_target_pairs={{0,1},{1,0},{2,3},{3,2},{4,5},{5,4},{6,7},{7,6},{8,9},{9,8},{10,11... | collective-permute-start | bytes 3145736 | tf_op jit(solution)/shard_map/ppermute | solution.py:73
  77.7 79.1 %collective-permute-start.11 = (bf16[16,80,512]{2,1,0:T(8,128)(2,1)}, bf16[16,80,512]{2,1,0:T(8,128)(2,1)}, u32[]{:S(2)}, u32[]{:S(2)}) collective-permute-start(bf16[16,80,512]{2,1,0:T(8,128)(2,1)} %bitcast.34), channel_id=1, source_target_pairs={{0,1},{1,0},{2,3},{3,2},{4,5},{5,4},{6,7},{7,6},{8,9},{9,8},{10,11... | collective-permute-start | bytes 3932168 | tf_op jit(solution)/shard_map/ppermute | solution.py:73
  97.8 65.1 %collective-permute-start.17 = (bf16[16,128,512]{2,1,0:T(8,128)(2,1)S(1)}, bf16[16,128,512]{2,1,0:T(8,128)(2,1)}, u32[]{:S(2)}, u32[]{:S(2)}) collective-permute-start(bf16[16,128,512]{2,1,0:T(8,128)(2,1)S(1)} %bitcast.259), channel_id=1, source_target_pairs={{0,1},{1,0},{2,3},{3,2},{4,5},{5,4},{6,7},{7,6},{8,9},{9,8},{10,11... | collective-permute-start | bytes 6291464 | tf_op jit(solution)/shard_map/ppermute | solution.py:73
  101.2 8.0 %copy-start.18 = (bf16[32,16,512]{2,1,0:T(8,128)(2,1)}, bf16[32,16,512]{2,1,0:T(8,128)(2,1)S(1)}, u32[]{:S(2)}) copy-start(bf16[32,16,512]{2,1,0:T(8,128)(2,1)S(1)} %get-tuple-element.78) | copy-start | bytes 1572868
  102.1 4.4 copy-start.30
  102.2 4.4 copy-start.20
  102.2 4.4 copy-start.32
  160.4 2.5 copy-start.6
  160.4 2.5 copy-start.13
  285.4 2.7 copy-start.3
  285.4 2.8 copy-start.31
  285.4 2.8 copy-start.29
  288.2 1.9 copy-start.11
  289.2 2.2 copy-start.27
  289.3 3.0 copy-start.10
  292.7 2.9 copy-start.9
  296.5 2.3 copy-start.17
  296.5 3.2 copy-start.16
  296.6 3.9 copy-start.15
  296.7 4.6 copy-start.26
  298.8 3.4 copy-start.25
  299.7 3.5 copy-start.24
  300.5 3.5 copy-start.23
  311.5 66.2 %collective-permute-start.24 = (bf16[16,224,512]{2,1,0:T(8,128)(2,1)}, bf16[16,224,512]{2,1,0:T(8,128)(2,1)}, u32[]{:S(2)}, u32[]{:S(2)}) collective-permute-start(bf16[16,224,512]{2,1,0:T(8,128)(2,1)} %dynamic-slice_bitcast_fusion), channel_id=1, source_target_pairs={{0,1},{1,0},{2,3},{3,2},{4,5},{5,4},{6,7},{7,6},{8,9},{9,8},{10,11... | collective-permute-start | bytes 11010056 | tf_op jit(solution)/shard_map/ppermute | solution.py:91
  365.4 2.2 copy-start.2
  368.5 3.7 copy-start.33
  372.2 1.6 copy-start.5
  375.1 2.7 slice-start
  375.4 3.0 slice-start.1
  375.4 9.4 %collective-permute-start.18 = (bf16[16,64,512]{2,1,0:T(8,128)(2,1)S(1)}, bf16[16,64,512]{2,1,0:T(8,128)(2,1)}, u32[]{:S(2)}, u32[]{:S(2)}) collective-permute-start(bf16[16,64,512]{2,1,0:T(8,128)(2,1)S(1)} %dynamic-slice_bitcast_fusion.2), channel_id=1, source_target_pairs={{0,1},{1,0},{2,3},{3,2},{4,5},{5,4},{6,7},{7,6},{8,9},{9,8},{10,11... | collective-permute-start | bytes 3145736 | tf_op jit(solution)/shard_map/ppermute | solution.py:91
  381.7 1.7 copy-start.21
  381.8 54.0 %collective-permute-start.25 = (bf16[8,224,512]{2,1,0:T(8,128)(2,1)S(1)}, bf16[8,224,512]{2,1,0:T(8,128)(2,1)S(1)}, u32[]{:S(2)}, u32[]{:S(2)}) collective-permute-start(bf16[8,224,512]{2,1,0:T(8,128)(2,1)S(1)} %dynamic-slice_bitcast_fusion.1), channel_id=1, source_target_pairs={{0,2},{1,3},{2,0},{3,1},{4,6},{5,7},{6,4},{7,5},{8,10},{9,11},{10,... | collective-permute-start | bytes 5505032 | tf_op jit(solution)/shard_map/ppermute | solution.py:91
  383.4 4.0 copy-start.8
  384.7 2.7 copy-start.4
  384.7 2.7 copy-start.19
  386.5 48.5 %collective-permute-start.19 = (bf16[8,64,512]{2,1,0:T(8,128)(2,1)S(1)}, bf16[8,64,512]{2,1,0:T(8,128)(2,1)S(1)}, u32[]{:S(2)}, u32[]{:S(2)}) collective-permute-start(bf16[8,64,512]{2,1,0:T(8,128)(2,1)S(1)} %dynamic-slice_bitcast_fusion.4), channel_id=1, source_target_pairs={{0,2},{1,3},{2,0},{3,1},{4,6},{5,7},{6,4},{7,5},{8,10},{9,11},{10,... | collective-permute-start | bytes 1572872 | tf_op jit(solution)/shard_map/ppermute | solution.py:91
  435.2 9.2 %collective-permute-start.20 = (bf16[4,64,512]{2,1,0:T(8,128)(2,1)S(1)}, bf16[4,64,512]{2,1,0:T(8,128)(2,1)S(1)}, u32[]{:S(2)}, u32[]{:S(2)}) collective-permute-start(bf16[4,64,512]{2,1,0:T(8,128)(2,1)S(1)} %dynamic-slice_bitcast_fusion.5), channel_id=1, source_target_pairs={{0,4},{1,5},{2,6},{3,7},{4,0},{5,1},{6,2},{7,3},{8,12},{9,13},{10,... | collective-permute-start | bytes 786440 | tf_op jit(solution)/shard_map/ppermute | solution.py:91
  436.4 1.7 copy-start.7
  436.4 1.7 copy-start.12
  436.5 11.4 %copy-start.14 = (bf16[32,16,512]{2,1,0:T(8,128)(2,1)S(1)}, bf16[32,16,512]{2,1,0:T(8,128)(2,1)}, u32[]{:S(2)}) copy-start(bf16[32,16,512]{2,1,0:T(8,128)(2,1)} %copy-done.13) | copy-start | bytes 1572868
  436.5 25.9 %collective-permute-start.26 = (bf16[4,224,512]{2,1,0:T(8,128)(2,1)S(1)}, bf16[4,224,512]{2,1,0:T(8,128)(2,1)S(1)}, u32[]{:S(2)}, u32[]{:S(2)}) collective-permute-start(bf16[4,224,512]{2,1,0:T(8,128)(2,1)S(1)} %dynamic-slice_bitcast_fusion.3), channel_id=1, source_target_pairs={{0,4},{1,5},{2,6},{3,7},{4,0},{5,1},{6,2},{7,3},{8,12},{9,13},{10,... | collective-permute-start | bytes 2752520 | tf_op jit(solution)/shard_map/ppermute | solution.py:91
  444.6 4.7 collective-permute-start.23
  444.7 5.2 %collective-permute-start.22 = (bf16[64,512]{1,0:T(8,128)(2,1)S(1)}, bf16[64,512]{1,0:T(8,128)(2,1)S(1)}, u32[]{:S(2)}, u32[]{:S(2)}) collective-permute-start(bf16[64,512]{1,0:T(8,128)(2,1)S(1)} %get-tuple-element.109), channel_id=1, source_target_pairs={{0,16},{1,17},{2,18},{3,19},{4,20},{5,21},{6,22},{7,23},{8,24},{9,... | collective-permute-start | bytes 196616 | tf_op jit(solution)/shard_map/ppermute | solution.py:98
  445.9 6.1 %collective-permute-start.21 = (bf16[64,512]{1,0:T(8,128)(2,1)S(1)}, bf16[64,512]{1,0:T(8,128)(2,1)S(1)}, u32[]{:S(2)}, u32[]{:S(2)}) collective-permute-start(bf16[64,512]{1,0:T(8,128)(2,1)S(1)} %get-tuple-element.107), channel_id=1, source_target_pairs={{0,8},{1,9},{2,10},{3,11},{4,12},{5,13},{6,14},{7,15},{8,16},{9,17... | collective-permute-start | bytes 196616 | tf_op jit(solution)/shard_map/ppermute | solution.py:98
  462.4 23.7 %copy-start.1 = (bf16[512,512]{1,0:T(8,128)(2,1)S(1)}, bf16[512,512]{1,0:T(8,128)(2,1)}, u32[]{:S(2)}) copy-start(bf16[512,512]{1,0:T(8,128)(2,1)} %param.28) | copy-start | bytes 1572868
  462.7 7.2 %collective-permute-start.29 = (bf16[224,512]{1,0:T(8,128)(2,1)S(1)}, bf16[224,512]{1,0:T(8,128)(2,1)S(1)}, u32[]{:S(2)}, u32[]{:S(2)}) collective-permute-start(bf16[224,512]{1,0:T(8,128)(2,1)S(1)} %get-tuple-element.91), channel_id=1, source_target_pairs={{0,24},{1,25},{2,26},{3,27},{4,28},{5,29},{6,30},{7,31},{8,0},{9,1... | collective-permute-start | bytes 688136 | tf_op jit(solution)/shard_map/ppermute | solution.py:98
  462.7 20.0 %collective-permute-start.28 = (bf16[224,512]{1,0:T(8,128)(2,1)S(1)}, bf16[224,512]{1,0:T(8,128)(2,1)S(1)}, u32[]{:S(2)}, u32[]{:S(2)}) collective-permute-start(bf16[224,512]{1,0:T(8,128)(2,1)S(1)} %get-tuple-element.92), channel_id=1, source_target_pairs={{0,16},{1,17},{2,18},{3,19},{4,20},{5,21},{6,22},{7,23},{8,24},{9,... | collective-permute-start | bytes 688136 | tf_op jit(solution)/shard_map/ppermute | solution.py:98
  464.0 18.7 %collective-permute-start.27 = (bf16[224,512]{1,0:T(8,128)(2,1)S(1)}, bf16[224,512]{1,0:T(8,128)(2,1)S(1)}, u32[]{:S(2)}, u32[]{:S(2)}) collective-permute-start(bf16[224,512]{1,0:T(8,128)(2,1)S(1)} %get-tuple-element.90), channel_id=1, source_target_pairs={{0,8},{1,9},{2,10},{3,11},{4,12},{5,13},{6,14},{7,15},{8,16},{9,17... | collective-permute-start | bytes 688136 | tf_op jit(solution)/shard_map/ppermute | solution.py:98
  (2 other events, 2.4 us)
